TPU v7x, 32 devices: a whole 2x2x4 slice. The times are simulated.
32 devices in a mesh: tile: 8 (over y, x, core), depth: 4 (over z).
Axes of the slice: x: 2, y: 2, z: 4, core: 2. Of those that a mesh axis runs over, the one named last changes fastest.
Arguments:
- samples: bfloat16 [4, 16, 4096, 128], P('depth', None, 'tile'), may hold values from -6 to 6
- opacity: float32 [4, 16, 4096], P('depth', None, 'tile'), may hold values from 0.004 to 0.06
- counts: int32 [4, 4096], P('depth', 'tile'), may hold values from 0 to 16
- depth_order: int32 [8, 4], P('tile'), may hold values from 0 to 3, each once within a row
- target: float32 [4096, 128], P(('tile', 'depth')), may hold values from -6 to 6
- weight_in: bfloat16 [4, 128, 256], P('depth'), may hold values from -0.5 to 0.5
- weight_out: bfloat16 [4, 256, 128], P('depth'), may hold values from -1.5 to 1.5
Outputs:
- pixels: float32 [4096, 128], P(('tile', 'depth'))
- grad_in: float32 [4, 128, 256], P('depth', 'tile')
- grad_out: float32 [4, 256, 128], P('depth', 'tile')
Inputs may be any that keep to these rules, and one draw needn't show every extreme that they name: `depth_order`: each row holds every brick rank 0 to 3 once.
All inputs are finite; a program needn't handle non-finite values.
Results may differ from a plain program's by a relative error of at most 0.0025.
Values sent between devices are 32-bit elements; how exact they have to be, the bound alone decides.
No kernel may reach another device: no remote copies, remote signals or barrier semaphores. Data moves between devices by JAX's collectives and lax.ppermute only.
A program may use at most 64 MiB of HBM per device.

v0:
```python
import jax
import jax.numpy as jnp
from jax import lax
from jax.sharding import PartitionSpec as P


def per_device(samples, opacity, counts, depth_order, target, weight_in, weight_out):
    inputs = samples[0]
    opaque = opacity[0]
    slot_total = opaque.shape[0]
    ray_total = opaque.shape[1]
    slot_index = lax.broadcasted_iota(jnp.int32, opaque.shape, 0)
    living = (slot_index < counts[0][None, :]).astype(jnp.float32)
    kept = 1.0 - opaque * living
    ones_row = jnp.ones((1, ray_total), jnp.float32)
    through = jnp.cumprod(jnp.concatenate([ones_row, kept[:-1]], axis=0), axis=0)
    contrib = living * opaque * through
    passing = jnp.prod(kept, axis=0)
    flat = inputs.reshape(slot_total * ray_total, inputs.shape[2])
    before_act = jnp.dot(flat, weight_in[0], preferred_element_type=jnp.float32)
    hidden = jnp.maximum(before_act, 0.0).astype(jnp.bfloat16)
    radiance = jnp.dot(hidden, weight_out[0], preferred_element_type=jnp.float32)
    radiance = radiance.reshape(slot_total, ray_total, radiance.shape[1])
    every_pass = lax.all_gather(passing[None, :], "depth", axis=0, tiled=True)
    brick_rank = depth_order[0]
    own_index = lax.axis_index("depth")
    picker = lax.broadcasted_iota(jnp.int32, brick_rank.shape, 0) == own_index
    own_rank = jnp.sum(jnp.where(picker, brick_rank, 0))
    in_front = brick_rank < own_rank
    veiling = jnp.prod(jnp.where(in_front[:, None], every_pass, 1.0), axis=0)
    factor = contrib * veiling[None, :]
    weighted = jnp.sum(factor[:, :, None] * radiance, axis=0)
    pixels = lax.psum_scatter(weighted, "depth", scatter_dimension=0, tiled=True)
    pixel_grad = lax.all_gather(pixels - target, "depth", axis=0, tiled=True)
    feat_grad = (factor[:, :, None] * pixel_grad[None, :, :]).astype(jnp.bfloat16)
    feat_grad = feat_grad.reshape(slot_total * ray_total, feat_grad.shape[2])
    grad_out = jnp.dot(hidden.T, feat_grad, preferred_element_type=jnp.float32)
    hidden_grad = jnp.dot(feat_grad, weight_out[0].T, preferred_element_type=jnp.float32)
    hidden_grad = jnp.where(before_act > 0.0, hidden_grad, 0.0).astype(jnp.bfloat16)
    grad_in = jnp.dot(flat.T, hidden_grad, preferred_element_type=jnp.float32)
    grad_in, grad_out = (
        lax.psum_scatter(grad_in, "tile", scatter_dimension=0, tiled=True),
        lax.psum_scatter(grad_out, "tile", scatter_dimension=0, tiled=True),
    )
    return (pixels, grad_in[None], grad_out[None])


def solution(mesh):
    placed = (
        P("depth", None, "tile", None),
        P("depth", None, "tile"),
        P("depth", "tile"),
        P("tile", None),
        P(("tile", "depth"), None),
        P("depth", None, None),
        P("depth", None, None),
    )
    return jax.shard_map(
        per_device,
        mesh=mesh,
        in_specs=placed,
        out_specs=(P(("tile", "depth"), None), P("depth", "tile", None), P("depth", "tile", None)),
        check_vma=False,
    )
```

profile of v0, /device:TPU:0, one launch (start us, length us, event | category | flops | bytes accessed | tf_op | source)
XLA Modules:
  0.0 157.2 jit_solution(14834239804294401704)
XLA Ops:
  7.2 0.0 copy-start
  7.2 0.0 reduce-scatter.6.cloned.1.call-start
  7.2 1.4 fusion.14
  8.7 1.3 bitcast_compare_fusion
  10.0 0.8 fusion.16
  10.7 13.6 %all-gather.1 = f32[4,1,512]{2,1,0:T(1,128)S(1)} all-gather(f32[1,1,512]{2,1,0:T(1,128)S(1)} %bitcast.74), channel_id=2, replica_groups=mesh['tile'=8,'depth'=4] {'depth'}, dimensions={0}, use_global_device_ids=true | all-gather | bytes 10240 | tf_op jit(solution)/shard_map/all_gather | solution.py:24
  24.4 0.1 fusion.13
  24.5 0.8 fusion.9
  25.3 0.0 copy-done
  25.3 0.0 copy-start.3
  25.3 5.3 %maximum_convert_fusion = (bf16[8192,256]{1,0:T(8,128)(2,1)S(1)}, f32[8192,256]{1,0:T(8,128)}) fusion(bf16[8192,128]{1,0:T(8,128)(2,1)S(1)} %bitcast.60, bf16[1,128,256]{2,1,0:T(8,128)(2,1)} %param.12), kind=kOutput, calls=%fused_computation.2 | convolution fusion | flops 541065216 | bytes 14745600 | tf_op jit(solution)/shard_map/dot_general | solution.py:20
  30.6 2.0 %copy-done.1 = bf16[8192,256]{1,0:T(8,128)(2,1)} copy-done((bf16[8192,256]{1,0:T(8,128)(2,1)}, bf16[8192,256]{1,0:T(8,128)(2,1)S(1)}, u32[]{:S(2)}) %copy-start.1) | copy-done | bytes 4194328
  32.6 0.0 copy-done.3
  32.6 2.2 %multiply_reduce_fusion = f32[512,128]{1,0:T(8,128)} fusion(bf16[16,512,256]{2,1,0:T(8,128)(2,1)S(1)} %bitcast.62, f32[16,512]{1,0:T(8,128)S(1)} %fusion.9, bf16[1,256,128]{2,1,0:T(8,128)(2,1)S(1)} %copy-done.3), kind=kOutput, calls=%fused_computation.6 | convolution fusion | flops 538902528 | bytes 4554752 | tf_op jit(solution)/shard_map/dot_general | solution.py:22
  34.9 0.0 reduce-scatter.6.cloned.1.call-update
  34.9 0.0 reduce-scatter.10.cloned.1.call-start
  35.0 0.0 copy-done.5
  35.1 19.7 %reduce-scatter.6.cloned.1.call-done = f32[128,128]{1,0:T(8,128)} async-done(((f32[512,128]{1,0:T(8,128)}), f32[128,128]{1,0:T(8,128)}) %reduce-scatter.6.cloned.1.call-update) | async-done | bytes 65552 | tf_op jit(solution)/shard_map/reduce_scatter | solution.py:33
  54.8 0.8 sub.11
  55.6 13.9 %all_gather.7 = f32[512,128]{1,0:T(8,128)S(1)} all-gather(f32[128,128]{1,0:T(8,128)S(1)} %sub.11), channel_id=1, replica_groups=mesh['tile'=8,'depth'=4] {'depth'}, dimensions={0}, use_global_device_ids=true | all-gather | bytes 327680 | tf_op jit(solution)/shard_map/all_gather | solution.py:34
  69.5 2.2 %multiply_convert_fusion = bf16[16,512,128]{2,1,0:T(8,128)(2,1)} fusion(f32[512,128]{1,0:T(8,128)S(1)} %all_gather.7, f32[16,512]{1,0:T(8,128)S(1)} %fusion.9), kind=kLoop, calls=%fused_computation.5 | loop fusion | flops 2097152 | bytes 2392064 | tf_op jit(solution)/shard_map/convert_element_type | solution.py:35
  71.7 2.2 %fusion.1 = bf16[8192,128]{1,0:T(8,128)(2,1)} fusion(f32[8192]{0:T(1024)S(1)} %multiply_multiply_fusion, f32[512,128]{1,0:T(8,128)S(1)} %all_gather.7), kind=kLoop, calls=%fused_computation.4 | loop fusion | flops 2097152 | bytes 2392064 | tf_op jit(solution)/shard_map/convert_element_type | solution.py:35
  73.9 6.6 %fusion.3 = f32[128,256]{0,1:T(8,128)S(1)} fusion(bf16[8192,128]{1,0:T(8,128)(2,1)S(1)} %bitcast.61, bf16[8192,128]{1,0:T(8,128)(2,1)} %bitcast.63, f32[8192,256]{1,0:T(8,128)} %get-tuple-element.12, bf16[1,256,128]{2,1,0:T(8,128)(2,1)S(1)} %copy-done.3), kind=kOutput, calls=%fused_computation.8 | convolution fusion | flops 1080033280 | bytes 12779520 | tf_op jit(solution)/shard_map/dot_general | solution.py:40
  80.5 0.7 copy.14
  81.2 0.0 reduce-scatter.10.cloned.1.call-update
  81.2 0.0 reduce-scatter.8.cloned.1.call-start
  81.3 4.8 %fusion.18 = f32[256,128]{1,0:T(8,128)} fusion(bf16[8192,256]{1,0:T(8,128)(2,1)} %copy-done.1, bf16[8192,128]{1,0:T(8,128)(2,1)} %fusion.1), kind=kOutput, calls=%fused_computation.30 | convolution fusion | flops 536870912 | bytes 6422528 | tf_op jit(solution)/shard_map/dot_general | solution.py:37
  86.1 0.0 reduce-scatter.8.cloned.1.call-update
  86.1 27.4 %reduce-scatter.10.cloned.1.call-done = f32[16,256]{1,0:T(8,128)} async-done(((f32[128,256]{1,0:T(8,128)}), f32[16,256]{1,0:T(8,128)}) %reduce-scatter.10.cloned.1.call-update) | async-done | bytes 16400
  113.5 0.8 copy.15
  114.3 0.7 copy.13
  115.0 35.7 %reduce-scatter.8.cloned.1.call-done = f32[32,128]{1,0:T(8,128)} async-done(((f32[256,128]{1,0:T(8,128)}), f32[32,128]{1,0:T(8,128)}) %reduce-scatter.8.cloned.1.call-update) | async-done | bytes 16400 | tf_op jit(solution)/shard_map/reduce_scatter | solution.py:43
  (14 shorter events, 0.1 us)
Async XLA Ops:
  7.2 18.1 %copy-start = (bf16[1,16,512,128]{3,2,1,0:T(8,128)(2,1)S(1)}, bf16[1,16,512,128]{3,2,1,0:T(8,128)(2,1)}, u32[]{:S(2)}) copy-start(bf16[1,16,512,128]{3,2,1,0:T(8,128)(2,1)} %param.7) | copy-start | bytes 6291460
  7.2 47.6 %reduce-scatter.6.cloned.1.call-start = ((), (), s32[]{:S(2)}) async-start(), calls=%async_computation.3 | async-start | bytes 327680 | tf_op jit(solution)/shard_map/reduce_scatter | solution.py:33
  25.3 7.3 %copy-start.3 = (bf16[1,256,128]{2,1,0:T(8,128)(2,1)S(1)}, bf16[1,256,128]{2,1,0:T(8,128)(2,1)}, u32[]{:S(2)}) copy-start(bf16[1,256,128]{2,1,0:T(8,128)(2,1)} %param.13) | copy-start | bytes 196612
  30.6 2.0 %copy-start.1 = (bf16[8192,256]{1,0:T(8,128)(2,1)}, bf16[8192,256]{1,0:T(8,128)(2,1)S(1)}, u32[]{:S(2)}) copy-start(bf16[8192,256]{1,0:T(8,128)(2,1)S(1)} %get-tuple-element.11) | copy-start | bytes 12582916
  30.6 4.3 %copy-start.2 = (f32[1,16,512]{2,1,0:T(8,128)S(1)}, f32[1,16,512]{2,1,0:T(8,128)}, u32[]{:S(2)}) copy-start(f32[1,16,512]{2,1,0:T(8,128)} %param.8) | copy-start | bytes 98308
  30.6 4.4 %copy-start.5 = (s32[1,512]{1,0:T(1,128)S(1)}, s32[1,512]{1,0:T(1,128)}, u32[]{:S(2)}) copy-start(s32[1,512]{1,0:T(1,128)} %param.9) | copy-start | bytes 6148
  30.6 24.1 %copy-start.4 = (f32[128,128]{1,0:T(8,128)S(1)}, f32[128,128]{1,0:T(8,128)}, u32[]{:S(2)}) copy-start(f32[128,128]{1,0:T(8,128)} %param.11) | copy-start | bytes 196612
  34.9 78.6 %reduce-scatter.10.cloned.1.call-start = ((), (), s32[]{:S(2)}) async-start(), calls=%async_computation.5 | async-start | bytes 147456
  81.2 69.5 %reduce-scatter.8.cloned.1.call-start = ((), (), s32[]{:S(2)}) async-start(), calls=%async_computation.4 | async-start | bytes 147456 | tf_op jit(solution)/shard_map/reduce_scatter | solution.py:43
Sparse Core Ops, SparseCore 0:
  35.0 19.7 reduce-scatter.5
  81.3 32.1 reduce-scatter.9
  117.1 33.5 reduce-scatter.7
where the time goes:
time: 158 us; the launch traced here: 157 us
  waiting for transfers between devices  82.8 us (52%)
  blocking collectives  27.5 us (17%)
  matrix products  19 us (12%)
  between operations  13.9 us (9%)
  other arithmetic  9.65 us (6%)
  local copies, waits for them, and re-layouts  4.29 us (3%)
    reduce_scatter x1, waiting for transfers between devices, per_device(): lax.psum_scatter(grad_out, 'tile', scatter_dimension=0, tiled=True)  35.7 us
    unnamed x4, waiting for transfers between devices  27.5 us
    reduce_scatter x1, waiting for transfers between devices, per_device(): lax.psum_scatter(weighted, 'depth', scatter_dimension=0, tiled=True)  19.7 us
    all_gather x1, blocking collectives, per_device(): pixel_grad = lax.all_gather(pixels - target, 'depth', axis=0, tiled=True)  13.9 us
    all_gather x1, blocking collectives, per_device(): every_pass = lax.all_gather(passing[None, :], 'depth', axis=0, tiled=True)  13.6 us
    dot_general x1, matrix products, per_device(): grad_in = jnp.dot(flat.T, hidden_grad, preferred_element_type=jnp.float32)  6.58 us
    dot_general x1, matrix products, per_device(): before_act = jnp.dot(flat, weight_in[0], preferred_element_type=jnp.float32)  5.32 us
    dot_general x1, matrix products, per_device(): grad_out = jnp.dot(hidden.T, feat_grad, preferred_element_type=jnp.float32)  4.82 us
  transfers between devices with their start and end apart: 3, of which 3 were waited for; matrix products, arithmetic and copies ran while one was open for 4% of the time, Pallas kernels for 0%

commit v1 on v0

v1 whole, which is shorter than its diff:
```python
import functools

import jax
import jax.numpy as jnp
from jax import lax
from jax.experimental import pallas as pl
from jax.experimental.pallas import tpu as pltpu
from jax.sharding import PartitionSpec as P

F32, BF16 = jnp.float32, jnp.bfloat16
VMEM = pl.BlockSpec(memory_space=pltpu.VMEM)
SMEM = pl.BlockSpec(memory_space=pltpu.SMEM)
PARAMS = pltpu.CompilerParams(vmem_limit_bytes=24 << 20)


def call(kernel, outs, *args, flops=0):
    return pl.pallas_call(
        kernel,
        out_shape=[jax.ShapeDtypeStruct(s, d) for s, d in outs],
        in_specs=[s for _, s in args],
        out_specs=[VMEM] * len(outs),
        compiler_params=PARAMS,
        cost_estimate=pl.CostEstimate(flops=flops, bytes_accessed=flops // 256, transcendentals=0),
    )(*[a for a, _ in args])


def split(value):
    high = value.astype(BF16)
    return high, (value - high.astype(F32)).astype(BF16)


def dot(a, b):
    return jnp.dot(a, b, preferred_element_type=F32)


def weights_kernel(opacity, counts, columns, passing):
    slots = opacity.shape[0]
    alive = lax.broadcasted_iota(jnp.int32, opacity.shape, 0) < counts[...]
    covered = jnp.where(alive, opacity[...], 0.0)
    kept = 1.0 - covered
    ones = jnp.ones_like(kept)
    through = jnp.concatenate([ones[:1], kept[:-1]], axis=0)
    step = 1
    while step < slots:
        through = through * jnp.concatenate([ones[:step], through[:-step]], axis=0)
        step *= 2
    columns[...] = (covered * through).T
    passing[...] = through[-1:] * kept[-1:]


def forward_kernel(chunks, own, samples, columns, passing, first, second, *outs):
    sent, kept = outs[: len(chunks)], outs[len(chunks) :]
    slots = samples.shape[0]
    for spot, k in enumerate(chunks):
        rows = sent[spot].shape[0] - 8
        chunk = own[0] ^ k
        start = pl.multiple_of(chunk * rows, rows)
        share = columns[pl.ds(start, rows), :]
        total = None
        for s in range(slots):
            active = jnp.maximum(dot(samples[s, pl.ds(start, rows), :], first[...]), 0.0)
            term = active * share[:, s : s + 1]
            total = term if total is None else total + term
        kept[spot][...] = total
        high, low = split(total)
        sent[spot][:rows] = dot(high, second[...]) + dot(low, second[...])
        line = jnp.zeros((1, rows), F32)
        for c in range(passing.shape[1] // rows):
            line = jnp.where(chunk == c, passing[:, c * rows : (c + 1) * rows], line)
        if rows < sent[spot].shape[1]:
            line = jnp.concatenate([line, jnp.zeros((1, sent[spot].shape[1] - rows), F32)], axis=1)
        sent[spot][rows:] = jnp.broadcast_to(line, (8, sent[spot].shape[1]))


def prepare_kernel(own, samples, columns, first, *rest):
    count = len(rest) - 4
    totals, (masked, turned, highs, lows) = rest[:count], rest[count:]
    slots = samples.shape[0]
    for k in range(count):
        rows = totals[k].shape[0]
        start = pl.multiple_of((own[0] ^ k) * rows, rows)
        share = columns[pl.ds(start, rows), :]
        for s in range(slots):
            block = samples[s, pl.ds(start, rows), :]
            active = dot(block, first[...])
            masked[k, s * rows : (s + 1) * rows] = jnp.where(active > 0.0, share[:, s : s + 1], 0.0).astype(BF16)
            turned[k, :, s * rows : (s + 1) * rows] = block.T
        high, low = split(totals[k][...].T)
        highs[k], lows[k] = high, low


def owner_kernel(own, ranks, target, *rest):
    count = (len(rest) - 1) // 2
    given, pixels, grads = rest[:count], rest[count], rest[count + 1 :]
    rows = target.shape[0]
    lines = [given[k][rows : rows + 1, :rows] for k in range(count)]
    rank = [ranks[0, own[0] ^ k] for k in range(count)]
    veils = []
    for k in range(count):
        veil = jnp.ones((1, rows), F32)
        for j in range(count):
            if j != k:
                veil = veil * jnp.where(rank[j] < rank[k], lines[j], 1.0)
        veils.append(veil)
    while len(veils) % 8:
        veils.append(veils[0])
    turned = jnp.concatenate(veils, axis=0).T
    total = None
    for k in range(count):
        term = given[k][:rows] * turned[:, k : k + 1]
        total = term if total is None else total + term
    pixels[...] = total
    slope = total - target[...]
    for k in range(count):
        grads[k][...] = slope * turned[:, k : k + 1]


def backward_terms(chunks, grads, masked, turned, highs, lows, second):
    inner = outer = None
    for spot, k in enumerate(chunks):
        high, low = split(grads[spot][...])
        rows = high.shape[0]
        across = (((1,), (1,)), ((), ()))
        back = lax.dot_general(high, second[...], across, preferred_element_type=F32)
        back = (back + lax.dot_general(low, second[...], across, preferred_element_type=F32)).astype(BF16)
        part = dot(highs[k], high) + dot(highs[k], low) + dot(lows[k], high)
        outer = part if outer is None else outer + part
        group = 2
        wide = jnp.concatenate([back] * group, axis=0)
        for j in range(0, masked.shape[1], group * rows):
            slope = masked[k, j : j + group * rows] * wide
            part = dot(turned[k, :, j : j + group * rows], slope)
            inner = part if inner is None else inner + part
    return inner, outer


def backward_kernel(chunks, masked, turned, highs, lows, second, *rest):
    grads, (inner, outer) = rest[: len(chunks)], rest[-2:]
    inner[...], outer[...] = backward_terms(chunks, grads, masked, turned, highs, lows, second)


def last_kernel(chunks, place, masked, turned, highs, lows, second, early_in, early_out, *rest):
    grads, (keep, send) = rest[: len(chunks)], rest[-2:]
    inner, outer = backward_terms(chunks, grads, masked, turned, highs, lows, second)
    inner, outer = inner + early_in[...], outer + early_out[...]
    pairs, width = keep.shape[0], keep.shape[2]
    few, many = inner.shape[0] // (2 * pairs), outer.shape[0] // (2 * pairs)
    even = place[0] % 2 == 0

    def put(a, at, one, two):
        size = one.shape[0]
        keep[a, at : at + size] = jnp.where(even, one, two)
        send[a, at : at + size] = jnp.where(even, two, one)

    for a in range(pairs):
        at = 0
        for c in range(0, inner.shape[1], width):
            put(a, at, *[inner[(2 * a + p) * few : (2 * a + p + 1) * few, c : c + width] for p in (0, 1)])
            at += few
        put(a, at, *[outer[(2 * a + p) * many : (2 * a + p + 1) * many] for p in (0, 1)])


def pair_kernel(place, keep, came, *outs):
    pair = place[0] // 2
    for k, out in enumerate(outs):
        out[...] = keep[pair ^ k] + came[pair ^ k]


def finish_kernel(*refs):
    given, (inner, outer) = refs[:-2], refs[-2:]
    total = given[0][...]
    for more in given[1:]:
        total = total + more[...]
    few, width = inner.shape[1], total.shape[1]
    for i, c in enumerate(range(0, inner.shape[2], width)):
        inner[0, :, c : c + width] = total[i * few : (i + 1) * few]
    outer[0] = total[few * (inner.shape[2] // width) :]


def per_device(bricks, tiles, samples, opacity, counts, depth_order, target, weight_in, weight_out):
    samples, opacity, weight_in, weight_out = samples[0], opacity[0], weight_in[0], weight_out[0]
    slots, rays, enc = samples.shape
    hid, feat = weight_out.shape
    rows = rays // bricks
    own = lax.axis_index("depth").astype(jnp.int32)[None]
    place = lax.axis_index("tile").astype(jnp.int32)[None]
    partner = lambda value, axis, size, k: lax.ppermute(value, axis, [(i, i ^ k) for i in range(size)])

    columns, passing = call(
        weights_kernel, [((rays, slots), F32), ((1, rays), F32)], (opacity, VMEM), (counts, VMEM)
    )
    order = list(range(bricks))
    out = call(
        functools.partial(forward_kernel, order),
        [((rows + 8, feat), F32)] * bricks + [((rows, hid), F32)] * bricks,
        (own, SMEM), (samples, VMEM), (columns, VMEM), (passing, VMEM), (weight_in, VMEM), (weight_out, VMEM),
        flops=2 * slots * rays * enc * hid,
    )
    sent, totals = out[:bricks], out[bricks:]
    came = [sent[0]] + [partner(sent[k], "depth", bricks, k) for k in range(1, bricks)]
    masked, turned, highs, lows = call(
        prepare_kernel,
        [
            ((bricks, slots * rows, hid), BF16),
            ((bricks, enc, slots * rows), BF16),
            ((bricks, hid, rows), BF16),
            ((bricks, hid, rows), BF16),
        ],
        (own, SMEM), (samples, VMEM), (columns, VMEM), (weight_in, VMEM), *[(t, VMEM) for t in totals],
        flops=2 * slots * rays * enc * hid,
    )
    out = call(
        owner_kernel,
        [((rows, feat), F32)] * (bricks + 1),
        (own, SMEM), (depth_order, SMEM), (target, VMEM), *[(c, VMEM) for c in came],
    )
    pixels, slopes = out[0], out[1:]
    grads = [slopes[0]] + [partner(slopes[k], "depth", bricks, k) for k in range(1, bricks)]
    saved = [(v, VMEM) for v in (masked, turned, highs, lows, weight_out)]
    early = [0]
    early_in, early_out = call(
        functools.partial(backward_kernel, early),
        [((enc, hid), F32), ((hid, feat), F32)],
        *saved, *[(grads[k], VMEM) for k in early],
        flops=2 * slots * rows * enc * hid,
    )
    late = [k for k in range(bricks) if k not in early]
    pairs = tiles // 2
    part = (enc * hid + hid * feat) // (tiles * feat)
    keep, send = call(
        functools.partial(last_kernel, late),
        [((pairs, part, feat), F32)] * 2,
        (place, SMEM), *saved, (early_in, VMEM), (early_out, VMEM), *[(grads[k], VMEM) for k in late],
        flops=2 * slots * rows * enc * hid * len(late),
    )
    other = partner(send, "tile", tiles, 1)
    parts = call(
        pair_kernel, [((part, feat), F32)] * pairs, (place, SMEM), (keep, VMEM), (other, VMEM)
    )
    parts = [parts[0]] + [partner(parts[k], "tile", tiles, 2 * k) for k in range(1, pairs)]
    grad_in, grad_out = call(
        finish_kernel,
        [((1, enc // tiles, hid), F32), ((1, hid // tiles, feat), F32)],
        *[(p, VMEM) for p in parts],
    )
    return pixels, grad_in, grad_out


def solution(mesh):
    bricks, tiles = mesh.shape["depth"], mesh.shape["tile"]
    placed = (
        P("depth", None, "tile", None),
        P("depth", None, "tile"),
        P("depth", "tile"),
        P("tile", None),
        P(("tile", "depth"), None),
        P("depth", None, None),
        P("depth", None, None),
    )
    return jax.shard_map(
        functools.partial(per_device, bricks, tiles),
        mesh=mesh,
        in_specs=placed,
        out_specs=(P(("tile", "depth"), None), P("depth", "tile", None), P("depth", "tile", None)),
        check_vma=False,
    )
```

time: 158 us -> 40.9 us (0.26)
  waiting for transfers between devices: 82.8 us -> 13.8 us
  blocking collectives: 27.5 us -> 0 us
  matrix products: 19 us -> 0 us
  starting transfers between devices: 0.12 us -> 13.7 us
  between operations: 13.9 us -> 0.75 us
  other arithmetic: 9.65 us -> 0 us
  Pallas kernels: 0 us -> 7.56 us
    reduce_scatter x2 -> x0, waiting for transfers between devices: 55.4 us -> none  [the longest x1 35.7 us: per_device(): lax.psum_scatter(grad_out, 'tile', scatter_dimension=0, tiled=True)]
    all_gather x2 -> x0, blocking collectives: 27.5 us -> none  [the longest x1 13.9 us: per_device(): pixel_grad = lax.all_gather(pixels - target, 'depth', axis=0, tiled=True)]
    unnamed x4 -> x0, waiting for transfers between devices: 27.5 us -> none
    dot_general x4 -> x0, matrix products: 19 us -> none  [the longest x1 6.58 us: per_device(): grad_in = jnp.dot(flat.T, hidden_grad, preferred_element_type=jnp.float32)]
    ppermute x0 -> x10, waiting for transfers between devices: none -> 13.8 us  [per_device(): lax.ppermute(value, axis, [(i, i ^ k) for i in range(size)])]
    ppermute x0 -> x10, starting transfers between devices: none -> 13.7 us  [per_device(): lax.ppermute(value, axis, [(i, i ^ k) for i in range(size)])]
    pallas_call x0 -> x8, Pallas kernels: none -> 7.56 us  [call(): pl.pallas_call(kernel, out_shape=[jax.ShapeDtypeStruct(s, d) for s, d in...]
    convert_element_type x2 -> x0, other arithmetic: 4.38 us -> none  [per_device(): (factor[:, :, None] * pixel_grad[None, :, :]).astype(jnp.bfloat16)]
  transfers between devices with their start and end apart: 3 -> 10, of which waited for: 3 -> 8; matrix products, arithmetic and copies ran while one was open for 4% -> 0% of each run, Pallas kernels for 0% -> 5%
where the time goes in v1:
time: 40.9 us; the launch traced here: 40.6 us
  waiting for transfers between devices  13.8 us (34%)
  starting transfers between devices  13.7 us (33%)
  Pallas kernels  7.56 us (18%)
  local copies, waits for them, and re-layouts  4.72 us (12%)
  between operations  0.75 us (2%)
    ppermute x10, waiting for transfers between devices, per_device(): lax.ppermute(value, axis, [(i, i ^ k) for i in range(size)])  13.8 us
    ppermute x10, starting transfers between devices, per_device(): lax.ppermute(value, axis, [(i, i ^ k) for i in range(size)])  13.7 us
    pallas_call x8, Pallas kernels, call(): pl.pallas_call(kernel, out_shape=[jax.ShapeDtypeStruct(s, d) for s, d in...  7.56 us
    unnamed x20, local copies, waits for them, and re-layouts  4.72 us
  transfers between devices with their start and end apart: 10, of which 8 were waited for; matrix products, arithmetic and copies ran while one was open for 0% of the time, Pallas kernels for 5%

profile of v1, /device:TPU:0, one launch (start us, length us, event | category | flops | bytes accessed | tf_op | source)
XLA Modules:
  0.0 40.6 jit_solution(14744114473287350731)
XLA Ops:
  0.7 0.7 %copy-done.7 = f32[1,16,512]{2,1,0:T(8,128)S(1)} copy-done((f32[1,16,512]{2,1,0:T(8,128)S(1)}, f32[1,16,512]{2,1,0:T(8,128)}, u32[]{:S(2)}) %copy-start.7) | copy-done | bytes 32792
  1.4 0.7 %copy-done.8 = s32[1,512]{1,0:T(1,128)S(1)} copy-done((s32[1,512]{1,0:T(1,128)S(1)}, s32[1,512]{1,0:T(1,128)}, u32[]{:S(2)}) %copy-start.8) | copy-done | bytes 2072
  2.1 0.1 shard_map.94
  2.2 0.0 copy-start
  2.2 1.6 %copy-done = bf16[1,16,512,128]{3,2,1,0:T(8,128)(2,1)S(1)} copy-done((bf16[1,16,512,128]{3,2,1,0:T(8,128)(2,1)S(1)}, bf16[1,16,512,128]{3,2,1,0:T(8,128)(2,1)}, u32[]{:S(2)}) %copy-start) | copy-done | bytes 2097176
  3.8 0.8 %copy-done.2 = bf16[1,256,128]{2,1,0:T(8,128)(2,1)S(1)} copy-done((bf16[1,256,128]{2,1,0:T(8,128)(2,1)S(1)}, bf16[1,256,128]{2,1,0:T(8,128)(2,1)}, u32[]{:S(2)}) %copy-start.2) | copy-done | bytes 65560
  4.7 0.8 %copy-done.4 = bf16[1,128,256]{2,1,0:T(8,128)(2,1)S(1)} copy-done((bf16[1,128,256]{2,1,0:T(8,128)(2,1)S(1)}, bf16[1,128,256]{2,1,0:T(8,128)(2,1)}, u32[]{:S(2)}) %copy-start.4) | copy-done | bytes 65560
  5.5 1.9 %shard_map.95 = (f32[136,128]{1,0:T(8,128)S(1)}, f32[136,128]{1,0:T(8,128)S(1)}, f32[136,128]{1,0:T(8,128)S(1)}, f32[136,128]{1,0:T(8,128)S(1)}, f32[128,256]{1,...) custom-call(s32[1]{0:T(128)} %bitcast.own, ...), custom_call_target="tpu_custom_call" | custom-call | flops 536870912 | bytes 2097152 | tf_op jit(solution)/shard_map/pallas_call | solution.py:17
  7.4 0.0 copy-start.3
  7.4 3.1 %collective-permute-start = (f32[136,128]{1,0:T(8,128)S(1)}, f32[136,128]{1,0:T(8,128)S(1)}, u32[]{:S(2)}, u32[]{:S(2)}) collective-permute-start(f32[136,128]{1,0:T(8,128)S(1)} %get-tuple-element.35), channel_id=1, source_target_pairs={{0,1},{1,0},{2,3},{3,2},{4,5},{5,4},{6,7},{7,6},{8,9},{9,8},{10,11... | collective-permute-start | bytes 208904 | tf_op jit(solution)/shard_map/ppermute | solution.py:187
  10.5 2.6 %collective-permute-start.1 = (f32[136,128]{1,0:T(8,128)S(1)}, f32[136,128]{1,0:T(8,128)S(1)}, u32[]{:S(2)}, u32[]{:S(2)}) collective-permute-start(f32[136,128]{1,0:T(8,128)S(1)} %get-tuple-element.36), channel_id=1, source_target_pairs={{0,2},{1,3},{2,0},{3,1},{4,6},{5,7},{6,4},{7,5},{8,10},{9,11},{10,... | collective-permute-start | bytes 208904 | tf_op jit(solution)/shard_map/ppermute | solution.py:187
  13.1 0.0 collective-permute-start.2
  13.1 4.9 %collective-permute-done.1.rest_2_ = f32[136,128]{1,0:T(8,128)S(1)} collective-permute-done((f32[136,128]{1,0:T(8,128)S(1)}, f32[136,128]{1,0:T(8,128)S(1)}, u32[]{:S(2)}, u32[]{:S(2)}) %collective-permute-start.1) | collective-permute-done | bytes 69664 | tf_op jit(solution)/shard_map/ppermute | solution.py:187
  18.1 1.3 %collective-permute-done.2.rest_3_ = f32[136,128]{1,0:T(8,128)S(1)} collective-permute-done((f32[136,128]{1,0:T(8,128)S(1)}, f32[136,128]{1,0:T(8,128)S(1)}, u32[]{:S(2)}, u32[]{:S(2)}) %collective-permute-start.2) | collective-permute-done | bytes 69664 | tf_op jit(solution)/shard_map/ppermute | solution.py:187
  19.3 1.4 %shard_map.96 = (f32[128,128]{1,0:T(8,128)}, f32[128,128]{1,0:T(8,128)S(1)}, f32[128,128]{1,0:T(8,128)S(1)}, f32[128,128]{1,0:T(8,128)S(1)}, f32[128,128]{1,0:T(8,128)S(1)}) custom-call(s32[1]{0:T(128)} %bitcast.own, s32[1,4]{1,0:T(1,128)S(1)} %copy-done.9, f32[128,128]{1,0:T(8,128)S(1)} %copy-done.6, f32[136,128]{1,0:T(8,128)S(1)} %get-tuple-element.34.rest_0_, ...), custom_call_target="tpu_custom_call" | custom-call | tf_op jit(solution)/shard_map/pallas_call | solution.py:17
  20.8 0.8 %collective-permute-start.3 = (f32[128,128]{1,0:T(8,128)S(1)}, f32[128,128]{1,0:T(8,128)S(1)}, u32[]{:S(2)}, u32[]{:S(2)}) collective-permute-start(f32[128,128]{1,0:T(8,128)S(1)} %get-tuple-element.50), channel_id=1, source_target_pairs={{0,1},{1,0},{2,3},{3,2},{4,5},{5,4},{6,7},{7,6},{8,9},{9,8},{10,11... | collective-permute-start | bytes 196616 | tf_op jit(solution)/shard_map/ppermute | solution.py:187
  21.6 1.7 %collective-permute-start.4 = (f32[128,128]{1,0:T(8,128)S(1)}, f32[128,128]{1,0:T(8,128)S(1)}, u32[]{:S(2)}, u32[]{:S(2)}) collective-permute-start(f32[128,128]{1,0:T(8,128)S(1)} %get-tuple-element.51), channel_id=1, source_target_pairs={{0,2},{1,3},{2,0},{3,1},{4,6},{5,7},{6,4},{7,5},{8,10},{9,11},{10,... | collective-permute-start | bytes 196616 | tf_op jit(solution)/shard_map/ppermute | solution.py:187
  23.3 1.9 %collective-permute-start.5 = (f32[128,128]{1,0:T(8,128)S(1)}, f32[128,128]{1,0:T(8,128)S(1)}, u32[]{:S(2)}, u32[]{:S(2)}) collective-permute-start(f32[128,128]{1,0:T(8,128)S(1)} %get-tuple-element.52), channel_id=1, source_target_pairs={{0,3},{1,2},{2,1},{3,0},{4,7},{5,6},{6,5},{7,4},{8,11},{9,10},{10,... | collective-permute-start | bytes 196616 | tf_op jit(solution)/shard_map/ppermute | solution.py:187
  25.2 1.6 %shard_map.97 = (bf16[4,2048,256]{2,1,0:T(8,128)(2,1)S(1)}, bf16[4,128,2048]{2,1,0:T(8,128)(2,1)S(1)}, bf16[4,256,128]{2,1,0:T(8,128)(2,1)S(1)}, bf16[4,256,128]{2,1,0:T(8,128)(2,1)S(1)}) custom-call(s32[1]{0:T(128)} %bitcast.own, bf16[16,512,128]{2,1,0:T(8,128)(2,1)S(1)} %bitcast.7, f32[512,16]{1,0:T(8,128)S(1)} %get-tuple-element.32.columns, ...), custom_call_target="tpu_custom_call" | custom-call | flops 536870912 | bytes 2097152 | tf_op jit(solution)/shard_map/pallas_call | solution.py:17
  26.8 0.6 %shard_map.98 = (f32[128,256]{1,0:T(8,128)S(1)}, f32[256,128]{1,0:T(8,128)S(1)}) custom-call(bf16[4,2048,256]{2,1,0:T(8,128)(2,1)S(1)} %get-tuple-element.43.masked, bf16[4,128,2048]{2,1,0:T(8,128)(2,1)S(1)} %get-tuple-element.44.turned, bf16[4,256,128]{2,1,0:T(8,128)(2,1)S(1)} %get-tuple-element.45.highs, bf16[4,256,128]{2,1,0:T(8,128)(2,1)S(1)} %get-tuple-element.46.lows, ...), custom_call_target="tpu_custom_call" | custom-call | flops 134217728 | bytes 524288 | tf_op jit(solution)/shard_map/pallas_call | solution.py:17
  27.4 0.3 collective-permute-done.4.rest_1_
  27.7 1.6 %collective-permute-done.5.rest_2_ = f32[128,128]{1,0:T(8,128)S(1)} collective-permute-done((f32[128,128]{1,0:T(8,128)S(1)}, f32[128,128]{1,0:T(8,128)S(1)}, u32[]{:S(2)}, u32[]{:S(2)}) %collective-permute-start.5) | collective-permute-done | bytes 65568 | tf_op jit(solution)/shard_map/ppermute | solution.py:187
  29.4 1.3 %shard_map.99 = (f32[4,64,128]{2,1,0:T(8,128)S(1)}, f32[4,64,128]{2,1,0:T(8,128)S(1)}) custom-call(s32[1]{0:T(128)} %bitcast.5.place, bf16[4,2048,256]{2,1,0:T(8,128)(2,1)S(1)} %get-tuple-element.43.masked, bf16[4,128,2048]{2,1,0:T(8,128)(2,1)S(1)} %get-tuple-element.44.turned, bf16[4,256,128]{2,1,0:T(8,128)(2,1)S(1)} %get-tuple-element.45.highs, ...), custom_call_target="tpu_custom_call" | custom-call | flops 402653184 | bytes 1572864 | tf_op jit(solution)/shard_map/pallas_call | solution.py:17
  30.6 0.1 collective-permute-start.6
  30.7 1.3 %collective-permute-done.6.came = f32[4,64,128]{2,1,0:T(8,128)S(1)} collective-permute-done((f32[4,64,128]{2,1,0:T(8,128)S(1)}, f32[4,64,128]{2,1,0:T(8,128)S(1)}, u32[]{:S(2)}, u32[]{:S(2)}) %collective-permute-start.6) | collective-permute-done | bytes 131104 | tf_op jit(solution)/shard_map/ppermute | solution.py:187
  32.1 1.6 %collective-permute-start.7 = (f32[64,128]{1,0:T(8,128)S(1)}, f32[64,128]{1,0:T(8,128)S(1)}, u32[]{:S(2)}, u32[]{:S(2)}) collective-permute-start(f32[64,128]{1,0:T(8,128)S(1)} %get-tuple-element.56), channel_id=1, source_target_pairs={{0,8},{4,12},{8,0},{12,4},{16,24},{20,28},{24,16},{28,20},{1,9},{5... | collective-permute-start | bytes 98312 | tf_op jit(solution)/shard_map/ppermute | solution.py:187
  33.6 1.5 %collective-permute-start.8 = (f32[64,128]{1,0:T(8,128)S(1)}, f32[64,128]{1,0:T(8,128)S(1)}, u32[]{:S(2)}, u32[]{:S(2)}) collective-permute-start(f32[64,128]{1,0:T(8,128)S(1)} %get-tuple-element.57), channel_id=1, source_target_pairs={{0,16},{4,20},{8,24},{12,28},{16,0},{20,4},{24,8},{28,12},{1,17},{... | collective-permute-start | bytes 98312 | tf_op jit(solution)/shard_map/ppermute | solution.py:187
  35.1 0.5 %collective-permute-start.9 = (f32[64,128]{1,0:T(8,128)S(1)}, f32[64,128]{1,0:T(8,128)S(1)}, u32[]{:S(2)}, u32[]{:S(2)}) collective-permute-start(f32[64,128]{1,0:T(8,128)S(1)} %get-tuple-element.58), channel_id=1, source_target_pairs={{0,24},{4,28},{8,16},{12,20},{16,8},{20,12},{24,0},{28,4},{1,25},{... | collective-permute-start | bytes 98312 | tf_op jit(solution)/shard_map/ppermute | solution.py:187
  35.6 0.4 %collective-permute-done.7.refs_1_ = f32[64,128]{1,0:T(8,128)S(1)} collective-permute-done((f32[64,128]{1,0:T(8,128)S(1)}, f32[64,128]{1,0:T(8,128)S(1)}, u32[]{:S(2)}, u32[]{:S(2)}) %collective-permute-start.7) | collective-permute-done | bytes 32800 | tf_op jit(solution)/shard_map/ppermute | solution.py:187
  36.0 1.5 %collective-permute-done.8.refs_2_ = f32[64,128]{1,0:T(8,128)S(1)} collective-permute-done((f32[64,128]{1,0:T(8,128)S(1)}, f32[64,128]{1,0:T(8,128)S(1)}, u32[]{:S(2)}, u32[]{:S(2)}) %collective-permute-start.8) | collective-permute-done | bytes 32800 | tf_op jit(solution)/shard_map/ppermute | solution.py:187
  37.5 2.4 %collective-permute-done.9.refs_3_ = f32[64,128]{1,0:T(8,128)S(1)} collective-permute-done((f32[64,128]{1,0:T(8,128)S(1)}, f32[64,128]{1,0:T(8,128)S(1)}, u32[]{:S(2)}, u32[]{:S(2)}) %collective-permute-start.9) | collective-permute-done | bytes 32800 | tf_op jit(solution)/shard_map/ppermute | solution.py:187
  40.0 0.6 %shard_map.101 = (f32[1,16,256]{2,1,0:T(8,128)}, f32[1,32,128]{2,1,0:T(8,128)}) custom-call(f32[64,128]{1,0:T(8,128)S(1)} %get-tuple-element.55.refs_0_, f32[64,128]{1,0:T(8,128)S(1)} %collective-permute-done.7.refs_1_, f32[64,128]{1,0:T(8,128)S(1)} %collective-permute-done.8.refs_2_, f32[64,128]{1,0:T(8,128)S(1)} %collective-permute-done.9.refs_3_), custom_call_target="tpu_custom_call" | custom-call | tf_op jit(solution)/shard_map/pallas_call | solution.py:17
  (16 shorter events, 0.0 us)
Async XLA Ops:
  0.6 18.7 %copy-start.9 = (s32[1,4]{1,0:T(1,128)S(1)}, s32[1,4]{1,0:T(1,128)}, u32[]{:S(2)}) copy-start(s32[1,4]{1,0:T(1,128)} %ranks.1) | copy-start | bytes 52
  0.6 0.8 %copy-start.7 = (f32[1,16,512]{2,1,0:T(8,128)S(1)}, f32[1,16,512]{2,1,0:T(8,128)}, u32[]{:S(2)}) copy-start(f32[1,16,512]{2,1,0:T(8,128)} %param.8) | copy-start | bytes 98308
  1.4 0.7 %copy-start.8 = (s32[1,512]{1,0:T(1,128)S(1)}, s32[1,512]{1,0:T(1,128)}, u32[]{:S(2)}) copy-start(s32[1,512]{1,0:T(1,128)} %counts.1) | copy-start | bytes 6148
  2.2 1.6 %copy-start = (bf16[1,16,512,128]{3,2,1,0:T(8,128)(2,1)S(1)}, bf16[1,16,512,128]{3,2,1,0:T(8,128)(2,1)}, u32[]{:S(2)}) copy-start(bf16[1,16,512,128]{3,2,1,0:T(8,128)(2,1)} %param.7) | copy-start | bytes 6291460
  3.8 0.8 %copy-start.2 = (bf16[1,256,128]{2,1,0:T(8,128)(2,1)S(1)}, bf16[1,256,128]{2,1,0:T(8,128)(2,1)}, u32[]{:S(2)}) copy-start(bf16[1,256,128]{2,1,0:T(8,128)(2,1)} %param.13) | copy-start | bytes 196612
  4.7 0.8 %copy-start.4 = (bf16[1,128,256]{2,1,0:T(8,128)(2,1)S(1)}, bf16[1,128,256]{2,1,0:T(8,128)(2,1)}, u32[]{:S(2)}) copy-start(bf16[1,128,256]{2,1,0:T(8,128)(2,1)} %param.12) | copy-start | bytes 196612
  5.5 13.8 %copy-start.6 = (f32[128,128]{1,0:T(8,128)S(1)}, f32[128,128]{1,0:T(8,128)}, u32[]{:S(2)}) copy-start(f32[128,128]{1,0:T(8,128)} %target.1) | copy-start | bytes 196612
  5.5 19.7 %copy-start.1 = (bf16[1,16,512,128]{3,2,1,0:T(8,128)(2,1)S(1)}, bf16[1,16,512,128]{3,2,1,0:T(8,128)(2,1)}, u32[]{:S(2)}) copy-start(bf16[1,16,512,128]{3,2,1,0:T(8,128)(2,1)} %param.7) | copy-start | bytes 6291460
  5.5 19.7 %copy-start.5 = (bf16[1,128,256]{2,1,0:T(8,128)(2,1)S(1)}, bf16[1,128,256]{2,1,0:T(8,128)(2,1)}, u32[]{:S(2)}) copy-start(bf16[1,128,256]{2,1,0:T(8,128)(2,1)} %param.12) | copy-start | bytes 196612
  7.4 19.4 %copy-start.3 = (bf16[1,256,128]{2,1,0:T(8,128)(2,1)S(1)}, bf16[1,256,128]{2,1,0:T(8,128)(2,1)}, u32[]{:S(2)}) copy-start(bf16[1,256,128]{2,1,0:T(8,128)(2,1)} %param.13) | copy-start | bytes 196612
  7.4 5.7 %collective-permute-start = (f32[136,128]{1,0:T(8,128)S(1)}, f32[136,128]{1,0:T(8,128)S(1)}, u32[]{:S(2)}, u32[]{:S(2)}) collective-permute-start(f32[136,128]{1,0:T(8,128)S(1)} %get-tuple-element.35), channel_id=1, source_target_pairs={{0,1},{1,0},{2,3},{3,2},{4,5},{5,4},{6,7},{7,6},{8,9},{9,8},{10,11... | collective-permute-start | bytes 208904 | tf_op jit(solution)/shard_map/ppermute | solution.py:187
  10.5 7.5 %collective-permute-start.1 = (f32[136,128]{1,0:T(8,128)S(1)}, f32[136,128]{1,0:T(8,128)S(1)}, u32[]{:S(2)}, u32[]{:S(2)}) collective-permute-start(f32[136,128]{1,0:T(8,128)S(1)} %get-tuple-element.36), channel_id=1, source_target_pairs={{0,2},{1,3},{2,0},{3,1},{4,6},{5,7},{6,4},{7,5},{8,10},{9,11},{10,... | collective-permute-start | bytes 208904 | tf_op jit(solution)/shard_map/ppermute | solution.py:187
  13.1 6.2 %collective-permute-start.2 = (f32[136,128]{1,0:T(8,128)S(1)}, f32[136,128]{1,0:T(8,128)S(1)}, u32[]{:S(2)}, u32[]{:S(2)}) collective-permute-start(f32[136,128]{1,0:T(8,128)S(1)} %get-tuple-element.37), channel_id=1, source_target_pairs={{0,3},{1,2},{2,1},{3,0},{4,7},{5,6},{6,5},{7,4},{8,11},{9,10},{10,... | collective-permute-start | bytes 208904 | tf_op jit(solution)/shard_map/ppermute | solution.py:187
  20.8 6.6 %collective-permute-start.3 = (f32[128,128]{1,0:T(8,128)S(1)}, f32[128,128]{1,0:T(8,128)S(1)}, u32[]{:S(2)}, u32[]{:S(2)}) collective-permute-start(f32[128,128]{1,0:T(8,128)S(1)} %get-tuple-element.50), channel_id=1, source_target_pairs={{0,1},{1,0},{2,3},{3,2},{4,5},{5,4},{6,7},{7,6},{8,9},{9,8},{10,11... | collective-permute-start | bytes 196616 | tf_op jit(solution)/shard_map/ppermute | solution.py:187
  21.6 6.2 %collective-permute-start.4 = (f32[128,128]{1,0:T(8,128)S(1)}, f32[128,128]{1,0:T(8,128)S(1)}, u32[]{:S(2)}, u32[]{:S(2)}) collective-permute-start(f32[128,128]{1,0:T(8,128)S(1)} %get-tuple-element.51), channel_id=1, source_target_pairs={{0,2},{1,3},{2,0},{3,1},{4,6},{5,7},{6,4},{7,5},{8,10},{9,11},{10,... | collective-permute-start | bytes 196616 | tf_op jit(solution)/shard_map/ppermute | solution.py:187
  23.3 6.1 %collective-permute-start.5 = (f32[128,128]{1,0:T(8,128)S(1)}, f32[128,128]{1,0:T(8,128)S(1)}, u32[]{:S(2)}, u32[]{:S(2)}) collective-permute-start(f32[128,128]{1,0:T(8,128)S(1)} %get-tuple-element.52), channel_id=1, source_target_pairs={{0,3},{1,2},{2,1},{3,0},{4,7},{5,6},{6,5},{7,4},{8,11},{9,10},{10,... | collective-permute-start | bytes 196616 | tf_op jit(solution)/shard_map/ppermute | solution.py:187
  30.6 1.4 %collective-permute-start.6 = (f32[4,64,128]{2,1,0:T(8,128)S(1)}, f32[4,64,128]{2,1,0:T(8,128)S(1)}, u32[]{:S(2)}, u32[]{:S(2)}) collective-permute-start(f32[4,64,128]{2,1,0:T(8,128)S(1)} %get-tuple-element.54), channel_id=1, source_target_pairs={{0,4},{4,0},{8,12},{12,8},{16,20},{20,16},{24,28},{28,24},{1,5},{5... | collective-permute-start | bytes 393224 | tf_op jit(solution)/shard_map/ppermute | solution.py:187
  32.1 4.0 %collective-permute-start.7 = (f32[64,128]{1,0:T(8,128)S(1)}, f32[64,128]{1,0:T(8,128)S(1)}, u32[]{:S(2)}, u32[]{:S(2)}) collective-permute-start(f32[64,128]{1,0:T(8,128)S(1)} %get-tuple-element.56), channel_id=1, source_target_pairs={{0,8},{4,12},{8,0},{12,4},{16,24},{20,28},{24,16},{28,20},{1,9},{5... | collective-permute-start | bytes 98312 | tf_op jit(solution)/shard_map/ppermute | solution.py:187
  33.6 3.9 %collective-permute-start.8 = (f32[64,128]{1,0:T(8,128)S(1)}, f32[64,128]{1,0:T(8,128)S(1)}, u32[]{:S(2)}, u32[]{:S(2)}) collective-permute-start(f32[64,128]{1,0:T(8,128)S(1)} %get-tuple-element.57), channel_id=1, source_target_pairs={{0,16},{4,20},{8,24},{12,28},{16,0},{20,4},{24,8},{28,12},{1,17},{... | collective-permute-start | bytes 98312 | tf_op jit(solution)/shard_map/ppermute | solution.py:187
  35.1 4.8 %collective-permute-start.9 = (f32[64,128]{1,0:T(8,128)S(1)}, f32[64,128]{1,0:T(8,128)S(1)}, u32[]{:S(2)}, u32[]{:S(2)}) collective-permute-start(f32[64,128]{1,0:T(8,128)S(1)} %get-tuple-element.58), channel_id=1, source_target_pairs={{0,24},{4,28},{8,16},{12,20},{16,8},{20,12},{24,0},{28,4},{1,25},{... | collective-permute-start | bytes 98312 | tf_op jit(solution)/shard_map/ppermute | solution.py:187

commit v2 on v1

v2 whole, which is shorter than its diff:
```python
import functools

import jax
import jax.numpy as jnp
from jax import lax
from jax.experimental import pallas as pl
from jax.experimental.pallas import tpu as pltpu
from jax.sharding import PartitionSpec as P

F32, BF16 = jnp.float32, jnp.bfloat16
VMEM = pl.BlockSpec(memory_space=pltpu.VMEM)
HBM = pl.BlockSpec(memory_space=pltpu.HBM)
SMEM = pl.BlockSpec(memory_space=pltpu.SMEM)


def call(kernel, outs, scalars, hbm, vmem, flops=0, scratch=(), grant=24):
    return pl.pallas_call(
        kernel,
        out_shape=[jax.ShapeDtypeStruct(s, d) for s, d in outs],
        in_specs=[SMEM] * len(scalars) + [HBM] * len(hbm) + [VMEM] * len(vmem),
        out_specs=[VMEM] * len(outs),
        scratch_shapes=scratch,
        compiler_params=pltpu.CompilerParams(vmem_limit_bytes=grant << 20),
        cost_estimate=pl.CostEstimate(flops=flops, bytes_accessed=flops // 256, transcendentals=0),
    )(*scalars, *[pltpu.with_memory_space_constraint(a, pltpu.HBM) for a in hbm], *vmem)


def split(value):
    high = value.astype(BF16)
    return high, (value - high.astype(F32)).astype(BF16)


def dot(a, b):
    return jnp.dot(a, b, preferred_element_type=F32)


def contributions(opacity, counts):
    slots = opacity.shape[0]
    alive = lax.broadcasted_iota(jnp.int32, opacity.shape, 0) < counts
    covered = jnp.where(alive, opacity, 0.0)
    kept = 1.0 - covered
    ones = jnp.ones_like(kept)
    through = jnp.concatenate([ones[:1], kept[:-1]], axis=0)
    step = 1
    while step < slots:
        through = through * jnp.concatenate([ones[:step], through[:-step]], axis=0)
        step *= 2
    return (covered * through).T, through[-1:] * kept[-1:]


def features(k, own, block, columns, passing, first, second, sent, kept):
    slots, rows, _ = block.shape
    chunk = own[0] ^ k
    share = columns[pl.ds(pl.multiple_of(chunk * rows, rows), rows), :]
    total = None
    for s in range(slots):
        term = jnp.maximum(dot(block[s], first[...]), 0.0) * share[:, s : s + 1]
        total = term if total is None else total + term
    kept[...] = total
    high, low = split(total)
    sent[:rows] = dot(high, second[...]) + dot(low, second[...])
    line = jnp.zeros((1, rows), F32)
    for c in range(passing.shape[1] // rows):
        line = jnp.where(chunk == c, passing[:, c * rows : (c + 1) * rows], line)
    if rows < sent.shape[1]:
        line = jnp.concatenate([line, jnp.zeros((1, sent.shape[1] - rows), F32)], axis=1)
    sent[rows:] = jnp.broadcast_to(line, (8, sent.shape[1]))


def load_kernel(chunks, rest, own, opacity, counts, samples, first, second, target, *refs):
    blocks, columns, passing, first_in, second_in, target_in = refs[:6]
    sent, kept = refs[6 : 6 + len(chunks)], refs[6 + len(chunks) : 6 + 2 * len(chunks)]
    opacity_in, counts_in, sems = refs[-3:]
    rows = blocks.shape[2]
    plain = [(opacity, opacity_in), (counts, counts_in), (first, first_in), (second, second_in), (target, target_in)]
    small = [pltpu.make_async_copy(a, b, sems.at[i]) for i, (a, b) in enumerate(plain)]
    large = {}
    for k in chunks + rest:
        start = pl.multiple_of((own[0] ^ k) * rows, rows)
        large[k] = pltpu.make_async_copy(samples.at[:, pl.ds(start, rows), :], blocks.at[k], sems.at[len(plain) + k])
    for copy in small[:3] + [large[k] for k in chunks] + small[3:4] + [large[k] for k in rest] + small[4:]:
        copy.start()
    small[0].wait()
    small[1].wait()
    columns[...], passing[...] = contributions(opacity_in[...], counts_in[...])
    small[2].wait()
    for spot, k in enumerate(chunks):
        large[k].wait()
        if spot == 0:
            small[3].wait()
        features(k, own, blocks.at[k], columns, passing, first_in, second_in, sent[spot], kept[spot])
    for k in rest:
        large[k].wait()
    small[4].wait()


def near_kernel(chunks, own, blocks, columns, passing, first, second, *outs):
    for spot, k in enumerate(chunks):
        sent, kept = outs[spot], outs[len(chunks) + spot]
        features(k, own, blocks.at[k], columns, passing, first, second, sent, kept)


def prepare_kernel(own, blocks, columns, first, *rest):
    count, slots, rows, _ = blocks.shape
    totals, (masked, turned, highs, lows) = rest[:count], rest[count:]
    for k in range(count):
        start = pl.multiple_of((own[0] ^ k) * rows, rows)
        share = columns[pl.ds(start, rows), :]
        for s in range(slots):
            block = blocks[k, s]
            active = dot(block, first[...])
            masked[k, s * rows : (s + 1) * rows] = jnp.where(active > 0.0, share[:, s : s + 1], 0.0).astype(BF16)
            turned[k, :, s * rows : (s + 1) * rows] = block.T
        highs[k], lows[k] = split(totals[k][...].T)


def owner_kernel(own, ranks, target, *rest):
    count = (len(rest) - 1) // 2
    given, pixels, grads = rest[:count], rest[count], rest[count + 1 :]
    rows = target.shape[0]
    lines = [given[k][rows : rows + 1, :rows] for k in range(count)]
    rank = [ranks[0, own[0] ^ k] for k in range(count)]
    veils = []
    for k in range(count):
        veil = jnp.ones((1, rows), F32)
        for j in range(count):
            if j != k:
                veil = veil * jnp.where(rank[j] < rank[k], lines[j], 1.0)
        veils.append(veil)
    while len(veils) % 8:
        veils.append(veils[0])
    turned = jnp.concatenate(veils, axis=0).T
    total = None
    for k in range(count):
        term = given[k][:rows] * turned[:, k : k + 1]
        total = term if total is None else total + term
    pixels[...] = total
    slope = total - target[...]
    for k in range(count):
        grads[k][...] = slope * turned[:, k : k + 1]


def backward_terms(chunks, grads, masked, turned, highs, lows, second):
    inner = outer = None
    for spot, k in enumerate(chunks):
        high, low = split(grads[spot][...])
        rows = high.shape[0]
        across = (((1,), (1,)), ((), ()))
        back = lax.dot_general(high, second[...], across, preferred_element_type=F32)
        back = (back + lax.dot_general(low, second[...], across, preferred_element_type=F32)).astype(BF16)
        part = dot(highs[k], high) + dot(highs[k], low) + dot(lows[k], high)
        outer = part if outer is None else outer + part
        group = 2
        wide = jnp.concatenate([back] * group, axis=0)
        for j in range(0, masked.shape[1], group * rows):
            slope = masked[k, j : j + group * rows] * wide
            part = dot(turned[k, :, j : j + group * rows], slope)
            inner = part if inner is None else inner + part
    return inner, outer


def backward_kernel(chunks, masked, turned, highs, lows, second, *rest):
    grads, before, (inner, outer) = rest[: len(chunks)], rest[len(chunks) : -2], rest[-2:]
    one, two = backward_terms(chunks, grads, masked, turned, highs, lows, second)
    inner[...], outer[...] = (one + before[0][...], two + before[1][...]) if before else (one, two)


def store_kernel(value, out):
    out[...] = value[...]


def last_kernel(chunks, place, masked, turned, highs, lows, second, early_in, early_out, *rest):
    grads, (keep, send) = rest[: len(chunks)], rest[-2:]
    inner, outer = backward_terms(chunks, grads, masked, turned, highs, lows, second)
    inner, outer = inner + early_in[...], outer + early_out[...]
    pairs, width = keep.shape[0], keep.shape[2]
    few, many = inner.shape[0] // (2 * pairs), outer.shape[0] // (2 * pairs)
    even = place[0] % 2 == 0

    def put(a, at, one, two):
        size = one.shape[0]
        keep[a, at : at + size] = jnp.where(even, one, two)
        send[a, at : at + size] = jnp.where(even, two, one)

    for a in range(pairs):
        at = 0
        for c in range(0, inner.shape[1], width):
            put(a, at, *[inner[(2 * a + p) * few : (2 * a + p + 1) * few, c : c + width] for p in (0, 1)])
            at += few
        put(a, at, *[outer[(2 * a + p) * many : (2 * a + p + 1) * many] for p in (0, 1)])


def pair_kernel(place, keep, came, *outs):
    pair = place[0] // 2
    for k, out in enumerate(outs):
        out[...] = keep[pair ^ k] + came[pair ^ k]


def finish_kernel(*refs):
    given, (inner, outer) = refs[:-2], refs[-2:]
    total = given[0][...]
    for more in given[1:]:
        total = total + more[...]
    few, width = inner.shape[1], total.shape[1]
    for i, c in enumerate(range(0, inner.shape[2], width)):
        inner[0, :, c : c + width] = total[i * few : (i + 1) * few]
    outer[0] = total[few * (inner.shape[2] // width) :]


def per_device(bricks, tiles, samples, opacity, counts, depth_order, target, weight_in, weight_out):
    return step(bricks, tiles, samples[0], opacity[0], counts, depth_order, target, weight_in[0], weight_out[0])


def partner(value, axis, size, k):
    return lax.ppermute(value, axis, [(i, i ^ k) for i in range(size)])


def step(bricks, tiles, samples, opacity, counts, depth_order, target, weight_in, weight_out):
    slots, rays, enc = samples.shape
    hid, feat = weight_out.shape
    rows = rays // bricks
    own = lax.axis_index("depth").astype(jnp.int32)[None]
    place = lax.axis_index("tile").astype(jnp.int32)[None]
    far = list(range(bricks - 1, bricks // 2 - 1, -1))
    near = list(range(bricks // 2 - 1, -1, -1))
    message, sums = ((rows + 8, feat), F32), ((rows, hid), F32)
    flops = 2 * slots * rows * enc * hid

    out = call(
        functools.partial(load_kernel, far, near),
        [
            ((bricks, slots, rows, enc), BF16),
            ((rays, slots), F32),
            ((1, rays), F32),
            (weight_in.shape, BF16),
            (weight_out.shape, BF16),
            (target.shape, F32),
        ]
        + [message] * len(far)
        + [sums] * len(far),
        [own],
        [opacity, counts, samples, weight_in, weight_out, target],
        [],
        flops=flops * len(far),
        scratch=[
            pltpu.VMEM(opacity.shape, F32),
            pltpu.VMEM(counts.shape, jnp.int32),
            pltpu.SemaphoreType.DMA((5 + bricks,)),
        ],
    )
    blocks, columns, passing, first, second, goal = out[:6]
    sent = dict(zip(far, out[6 : 6 + len(far)]))
    totals = dict(zip(far, out[6 + len(far) :]))
    came = {k: partner(sent[k], "depth", bricks, k) for k in far}
    out = call(
        functools.partial(near_kernel, near),
        [message] * len(near) + [sums] * len(near),
        [own],
        [],
        [blocks, columns, passing, first, second],
        flops=flops * len(near),
    )
    sent.update(zip(near, out[: len(near)]))
    totals.update(zip(near, out[len(near) :]))
    came.update({k: partner(sent[k], "depth", bricks, k) if k else sent[k] for k in near})
    masked, turned, highs, lows = call(
        prepare_kernel,
        [
            ((bricks, slots * rows, hid), BF16),
            ((bricks, enc, slots * rows), BF16),
            ((bricks, hid, rows), BF16),
            ((bricks, hid, rows), BF16),
        ],
        [own],
        [],
        [blocks, columns, first] + [totals[k] for k in range(bricks)],
        flops=flops * bricks,
    )
    out = call(
        owner_kernel,
        [((rows, feat), F32)] * (bricks + 1),
        [own, depth_order],
        [],
        [goal] + [came[k] for k in range(bricks)],
    )
    slopes = dict(enumerate(out[1:]))
    grads = {k: partner(slopes[k], "depth", bricks, k) if k else slopes[k] for k in far + near}
    (pixels,) = call(store_kernel, [((rows, feat), F32)], [], [], [out[0]])

    saved = [masked, turned, highs, lows, second]
    gradients = [((enc, hid), F32), ((hid, feat), F32)]
    before = []
    for k in reversed(near):
        before = call(
            functools.partial(backward_kernel, [k]), gradients, [], [], saved + [grads[k]] + list(before), flops=flops
        )
    pairs = tiles // 2
    part = (enc * hid + hid * feat) // (tiles * feat)
    keep, send = call(
        functools.partial(last_kernel, far),
        [((pairs, part, feat), F32)] * 2,
        [place],
        [],
        saved + list(before) + [grads[k] for k in far],
        flops=flops * len(far),
    )
    other = partner(send, "tile", tiles, 1)
    parts = call(pair_kernel, [((part, feat), F32)] * pairs, [place], [], [keep, other])
    parts = [partner(parts[k], "tile", tiles, 2 * k) if k else parts[k] for k in range(pairs - 1, -1, -1)]
    grad_in, grad_out = call(
        finish_kernel, [((1, enc // tiles, hid), F32), ((1, hid // tiles, feat), F32)], [], [], parts
    )
    return pixels, grad_in, grad_out


def solution(mesh):
    bricks, tiles = mesh.shape["depth"], mesh.shape["tile"]
    placed = (
        P("depth", None, "tile", None),
        P("depth", None, "tile"),
        P("depth", "tile"),
        P("tile", None),
        P(("tile", "depth"), None),
        P("depth", None, None),
        P("depth", None, None),
    )
    return jax.shard_map(
        functools.partial(per_device, bricks, tiles),
        mesh=mesh,
        in_specs=placed,
        out_specs=(P(("tile", "depth"), None), P("depth", "tile", None), P("depth", "tile", None)),
        check_vma=False,
    )
```

time: 40.9 us -> 35.1 us (0.86)
  local copies, waits for them, and re-layouts: 4.72 us -> 0.01 us
  waiting for transfers between devices: 13.8 us -> 11.8 us
  Pallas kernels: 7.56 us -> 9.33 us
  starting transfers between devices: 13.7 us -> 13.1 us
    unnamed x20 -> x2, local copies, waits for them, and re-layouts: 4.72 us -> 0.01 us
    ppermute x10, waiting for transfers between devices: 13.8 us -> 11.8 us  [partner(): return lax.ppermute(value, axis, [(i, i ^ k) for i in range(size)])]
    pallas_call x8 -> x10, Pallas kernels: 7.56 us -> 9.33 us  [call(): pl.pallas_call(kernel, out_shape=[jax.ShapeDtypeStruct(s, d) for s, d in...]
    ppermute x10, starting transfers between devices: 13.7 us -> 13.1 us  [partner(): return lax.ppermute(value, axis, [(i, i ^ k) for i in range(size)])]
  transfers between devices with their start and end apart: 10 -> 10, of which waited for: 8 -> 9; matrix products, arithmetic and copies ran while one was open for 0% -> 0% of each run, Pallas kernels for 5% -> 13%
where the time goes in v2:
time: 35.1 us; the launch traced here: 35 us
  starting transfers between devices  13.1 us (37%)
  waiting for transfers between devices  11.8 us (34%)
  Pallas kernels  9.33 us (27%)
  between operations  0.72 us (2%)
    ppermute x10, starting transfers between devices, partner(): return lax.ppermute(value, axis, [(i, i ^ k) for i in range(size)])  13.1 us
    ppermute x10, waiting for transfers between devices, partner(): return lax.ppermute(value, axis, [(i, i ^ k) for i in range(size)])  11.8 us
    pallas_call x10, Pallas kernels, call(): pl.pallas_call(kernel, out_shape=[jax.ShapeDtypeStruct(s, d) for s, d in...  9.33 us
  transfers between devices with their start and end apart: 10, of which 9 were waited for; matrix products, arithmetic and copies ran while one was open for 0% of the time, Pallas kernels for 13%

profile of v2, /device:TPU:0, one launch (start us, length us, event | category | flops | bytes accessed | tf_op | source)
XLA Modules:
  0.0 35.0 jit_solution(9590977075559938700)
XLA Ops:
  0.6 0.0 copy-start
  0.6 2.5 %shard_map.94 = (bf16[4,16,128,128]{3,2,1,0:T(8,128)(2,1)S(1)}, f32[512,16]{1,0:T(8,128)S(1)}, f32[1,512]{1,0:T(1,128)S(1)}, bf16[128,256]{1,0:T(8,128)(2,1)S(1)...) custom-call(s32[1]{0:T(128)} %bitcast.own, ...), custom_call_target="tpu_custom_call" | custom-call | flops 268435456 | bytes 1048576 | tf_op jit(solution)/shard_map/pallas_call | solution.py:17
  3.1 4.1 %collective-permute-start.1 = (f32[136,128]{1,0:T(8,128)S(1)}, f32[136,128]{1,0:T(8,128)S(1)}, u32[]{:S(2)}, u32[]{:S(2)}) collective-permute-start(f32[136,128]{1,0:T(8,128)S(1)} %get-tuple-element.46), channel_id=1, source_target_pairs={{0,2},{1,3},{2,0},{3,1},{4,6},{5,7},{6,4},{7,5},{8,10},{9,11},{10,... | collective-permute-start | bytes 208904 | tf_op jit(solution)/shard_map/ppermute | solution.py:215
  7.3 1.3 %collective-permute-start.2 = (f32[136,128]{1,0:T(8,128)S(1)}, f32[136,128]{1,0:T(8,128)S(1)}, u32[]{:S(2)}, u32[]{:S(2)}) collective-permute-start(f32[136,128]{1,0:T(8,128)S(1)} %get-tuple-element.47), channel_id=1, source_target_pairs={{0,3},{1,2},{2,1},{3,0},{4,7},{5,6},{6,5},{7,4},{8,11},{9,10},{10,... | collective-permute-start | bytes 208904 | tf_op jit(solution)/shard_map/ppermute | solution.py:215
  8.6 1.0 %shard_map.95 = (f32[136,128]{1,0:T(8,128)S(1)}, f32[136,128]{1,0:T(8,128)S(1)}, f32[128,256]{1,0:T(8,128)S(1)}, f32[128,256]{1,0:T(8,128)S(1)}) custom-call(s32[1]{0:T(128)} %bitcast.own, bf16[4,16,128,128]{3,2,1,0:T(8,128)(2,1)S(1)} %get-tuple-element.39.blocks, f32[512,16]{1,0:T(8,128)S(1)} %get-tuple-element.40.columns, ...), custom_call_target="tpu_custom_call" | custom-call | flops 268435456 | bytes 1048576 | tf_op jit(solution)/shard_map/pallas_call | solution.py:17
  9.6 0.3 collective-permute-start
  9.9 1.3 %collective-permute-done.1.rest_2_ = f32[136,128]{1,0:T(8,128)S(1)} collective-permute-done((f32[136,128]{1,0:T(8,128)S(1)}, f32[136,128]{1,0:T(8,128)S(1)}, u32[]{:S(2)}, u32[]{:S(2)}) %collective-permute-start.1) | collective-permute-done | bytes 69664 | tf_op jit(solution)/shard_map/ppermute | solution.py:215
  11.2 2.9 %collective-permute-done.2.rest_3_ = f32[136,128]{1,0:T(8,128)S(1)} collective-permute-done((f32[136,128]{1,0:T(8,128)S(1)}, f32[136,128]{1,0:T(8,128)S(1)}, u32[]{:S(2)}, u32[]{:S(2)}) %collective-permute-start.2) | collective-permute-done | bytes 69664 | tf_op jit(solution)/shard_map/ppermute | solution.py:215
  14.1 0.3 collective-permute-done.rest_1_
  14.4 0.0 copy-done
  14.4 0.8 %shard_map.96 = (f32[128,128]{1,0:T(8,128)S(1)}, f32[128,128]{1,0:T(8,128)S(1)}, f32[128,128]{1,0:T(8,128)S(1)}, f32[128,128]{1,0:T(8,128)S(1)}, f32[128,128]{1,0:T(8,128)S(1)}) custom-call(s32[1]{0:T(128)} %bitcast.own, s32[1,4]{1,0:T(1,128)S(1)} %copy-done, f32[128,128]{1,0:T(8,128)S(1)} %get-tuple-element.38.target, ...), custom_call_target="tpu_custom_call" | custom-call | tf_op jit(solution)/shard_map/pallas_call | solution.py:17
  15.2 0.3 collective-permute-start.3
  15.6 3.4 %collective-permute-start.4 = (f32[128,128]{1,0:T(8,128)S(1)}, f32[128,128]{1,0:T(8,128)S(1)}, u32[]{:S(2)}, u32[]{:S(2)}) collective-permute-start(f32[128,128]{1,0:T(8,128)S(1)} %get-tuple-element.63), channel_id=1, source_target_pairs={{0,3},{1,2},{2,1},{3,0},{4,7},{5,6},{6,5},{7,4},{8,11},{9,10},{10,... | collective-permute-start | bytes 196616 | tf_op jit(solution)/shard_map/ppermute | solution.py:215
  19.0 0.0 collective-permute-start.5
  19.0 1.6 %shard_map.98 = (bf16[4,2048,256]{2,1,0:T(8,128)(2,1)S(1)}, bf16[4,128,2048]{2,1,0:T(8,128)(2,1)S(1)}, bf16[4,256,128]{2,1,0:T(8,128)(2,1)S(1)}, bf16[4,256,128]{2,1,0:T(8,128)(2,1)S(1)}) custom-call(s32[1]{0:T(128)} %bitcast.own, bf16[4,16,128,128]{3,2,1,0:T(8,128)(2,1)S(1)} %get-tuple-element.39.blocks, f32[512,16]{1,0:T(8,128)S(1)} %get-tuple-element.40.columns, ...), custom_call_target="tpu_custom_call" | custom-call | flops 536870912 | bytes 2097152 | tf_op jit(solution)/shard_map/pallas_call | solution.py:17
  20.6 0.6 %shard_map.99 = (f32[128,256]{1,0:T(8,128)S(1)}, f32[256,128]{1,0:T(8,128)S(1)}) custom-call(bf16[4,2048,256]{2,1,0:T(8,128)(2,1)S(1)} %get-tuple-element.53.masked, bf16[4,128,2048]{2,1,0:T(8,128)(2,1)S(1)} %get-tuple-element.54.turned, bf16[4,256,128]{2,1,0:T(8,128)(2,1)S(1)} %get-tuple-element.55.highs, bf16[4,256,128]{2,1,0:T(8,128)(2,1)S(1)} %get-tuple-element.56.lows, ...), custom_call_target="tpu_custom_call" | custom-call | flops 134217728 | bytes 524288 | tf_op jit(solution)/shard_map/pallas_call | solution.py:17
  21.2 0.0 collective-permute-done.3.rest_0_
  21.2 0.6 %shard_map.100 = (f32[128,256]{1,0:T(8,128)S(1)}, f32[256,128]{1,0:T(8,128)S(1)}) custom-call(bf16[4,2048,256]{2,1,0:T(8,128)(2,1)S(1)} %get-tuple-element.53.masked, bf16[4,128,2048]{2,1,0:T(8,128)(2,1)S(1)} %get-tuple-element.54.turned, bf16[4,256,128]{2,1,0:T(8,128)(2,1)S(1)} %get-tuple-element.55.highs, bf16[4,256,128]{2,1,0:T(8,128)(2,1)S(1)} %get-tuple-element.56.lows, ...), custom_call_target="tpu_custom_call" | custom-call | flops 134217728 | bytes 524288 | tf_op jit(solution)/shard_map/pallas_call | solution.py:17
  21.8 0.7 %collective-permute-done.4.rest_0_ = f32[128,128]{1,0:T(8,128)S(1)} collective-permute-done((f32[128,128]{1,0:T(8,128)S(1)}, f32[128,128]{1,0:T(8,128)S(1)}, u32[]{:S(2)}, u32[]{:S(2)}) %collective-permute-start.4) | collective-permute-done | bytes 65568 | tf_op jit(solution)/shard_map/ppermute | solution.py:215
  22.5 2.5 %collective-permute-done.5.rest_1_ = f32[128,128]{1,0:T(8,128)S(1)} collective-permute-done((f32[128,128]{1,0:T(8,128)S(1)}, f32[128,128]{1,0:T(8,128)S(1)}, u32[]{:S(2)}, u32[]{:S(2)}) %collective-permute-start.5) | collective-permute-done | bytes 65568 | tf_op jit(solution)/shard_map/ppermute | solution.py:215
  25.0 1.0 %shard_map.101 = (f32[4,64,128]{2,1,0:T(8,128)S(1)}, f32[4,64,128]{2,1,0:T(8,128)S(1)}) custom-call(s32[1]{0:T(128)} %bitcast.5.place, bf16[4,2048,256]{2,1,0:T(8,128)(2,1)S(1)} %get-tuple-element.53.masked, bf16[4,128,2048]{2,1,0:T(8,128)(2,1)S(1)} %get-tuple-element.54.turned, bf16[4,256,128]{2,1,0:T(8,128)(2,1)S(1)} %get-tuple-element.55.highs, ...), custom_call_target="tpu_custom_call" | custom-call | flops 268435456 | bytes 1048576 | tf_op jit(solution)/shard_map/pallas_call | solution.py:17
  26.0 0.1 collective-permute-start.6
  26.1 1.3 %collective-permute-done.6.came = f32[4,64,128]{2,1,0:T(8,128)S(1)} collective-permute-done((f32[4,64,128]{2,1,0:T(8,128)S(1)}, f32[4,64,128]{2,1,0:T(8,128)S(1)}, u32[]{:S(2)}, u32[]{:S(2)}) %collective-permute-start.6) | collective-permute-done | bytes 131104 | tf_op jit(solution)/shard_map/ppermute | solution.py:215
  27.4 2.5 %collective-permute-start.7 = (f32[64,128]{1,0:T(8,128)S(1)}, f32[64,128]{1,0:T(8,128)S(1)}, u32[]{:S(2)}, u32[]{:S(2)}) collective-permute-start(f32[64,128]{1,0:T(8,128)S(1)} %get-tuple-element.67), channel_id=1, source_target_pairs={{0,24},{4,28},{8,16},{12,20},{16,8},{20,12},{24,0},{28,4},{1,25},{... | collective-permute-start | bytes 98312 | tf_op jit(solution)/shard_map/ppermute | solution.py:215
  29.9 0.5 %collective-permute-start.8 = (f32[64,128]{1,0:T(8,128)S(1)}, f32[64,128]{1,0:T(8,128)S(1)}, u32[]{:S(2)}, u32[]{:S(2)}) collective-permute-start(f32[64,128]{1,0:T(8,128)S(1)} %get-tuple-element.68), channel_id=1, source_target_pairs={{0,16},{4,20},{8,24},{12,28},{16,0},{20,4},{24,8},{28,12},{1,17},{... | collective-permute-start | bytes 98312 | tf_op jit(solution)/shard_map/ppermute | solution.py:215
  30.4 0.5 %collective-permute-start.9 = (f32[64,128]{1,0:T(8,128)S(1)}, f32[64,128]{1,0:T(8,128)S(1)}, u32[]{:S(2)}, u32[]{:S(2)}) collective-permute-start(f32[64,128]{1,0:T(8,128)S(1)} %get-tuple-element.69), channel_id=1, source_target_pairs={{0,8},{4,12},{8,0},{12,4},{16,24},{20,28},{24,16},{28,20},{1,9},{5... | collective-permute-start | bytes 98312 | tf_op jit(solution)/shard_map/ppermute | solution.py:215
  31.0 0.6 %shard_map.97 = f32[128,128]{1,0:T(8,128)} custom-call(f32[128,128]{1,0:T(8,128)S(1)} %get-tuple-element.48.value), custom_call_target="tpu_custom_call" | custom-call | tf_op jit(solution)/shard_map/pallas_call | solution.py:17
  31.6 0.7 %collective-permute-done.7.refs_0_ = f32[64,128]{1,0:T(8,128)S(1)} collective-permute-done((f32[64,128]{1,0:T(8,128)S(1)}, f32[64,128]{1,0:T(8,128)S(1)}, u32[]{:S(2)}, u32[]{:S(2)}) %collective-permute-start.7) | collective-permute-done | bytes 32800 | tf_op jit(solution)/shard_map/ppermute | solution.py:215
  32.3 1.6 %collective-permute-done.8.refs_1_ = f32[64,128]{1,0:T(8,128)S(1)} collective-permute-done((f32[64,128]{1,0:T(8,128)S(1)}, f32[64,128]{1,0:T(8,128)S(1)}, u32[]{:S(2)}, u32[]{:S(2)}) %collective-permute-start.8) | collective-permute-done | bytes 32800 | tf_op jit(solution)/shard_map/ppermute | solution.py:215
  33.9 0.5 %collective-permute-done.9.refs_2_ = f32[64,128]{1,0:T(8,128)S(1)} collective-permute-done((f32[64,128]{1,0:T(8,128)S(1)}, f32[64,128]{1,0:T(8,128)S(1)}, u32[]{:S(2)}, u32[]{:S(2)}) %collective-permute-start.9) | collective-permute-done | bytes 32800 | tf_op jit(solution)/shard_map/ppermute | solution.py:215
  34.4 0.6 %shard_map.103 = (f32[1,16,256]{2,1,0:T(8,128)}, f32[1,32,128]{2,1,0:T(8,128)}) custom-call(f32[64,128]{1,0:T(8,128)S(1)} %collective-permute-done.7.refs_0_, f32[64,128]{1,0:T(8,128)S(1)} %collective-permute-done.8.refs_1_, f32[64,128]{1,0:T(8,128)S(1)} %collective-permute-done.9.refs_2_, f32[64,128]{1,0:T(8,128)S(1)} %get-tuple-element.70.refs_3_), custom_call_target="tpu_custom_call" | custom-call | tf_op jit(solution)/shard_map/pallas_call | solution.py:17
  (1 shorter events, 0.0 us)
Async XLA Ops:
  0.6 13.8 %copy-start = (s32[1,4]{1,0:T(1,128)S(1)}, s32[1,4]{1,0:T(1,128)}, u32[]{:S(2)}) copy-start(s32[1,4]{1,0:T(1,128)} %ranks.1) | copy-start | bytes 52
  3.1 8.1 %collective-permute-start.1 = (f32[136,128]{1,0:T(8,128)S(1)}, f32[136,128]{1,0:T(8,128)S(1)}, u32[]{:S(2)}, u32[]{:S(2)}) collective-permute-start(f32[136,128]{1,0:T(8,128)S(1)} %get-tuple-element.46), channel_id=1, source_target_pairs={{0,2},{1,3},{2,0},{3,1},{4,6},{5,7},{6,4},{7,5},{8,10},{9,11},{10,... | collective-permute-start | bytes 208904 | tf_op jit(solution)/shard_map/ppermute | solution.py:215
  7.3 6.8 %collective-permute-start.2 = (f32[136,128]{1,0:T(8,128)S(1)}, f32[136,128]{1,0:T(8,128)S(1)}, u32[]{:S(2)}, u32[]{:S(2)}) collective-permute-start(f32[136,128]{1,0:T(8,128)S(1)} %get-tuple-element.47), channel_id=1, source_target_pairs={{0,3},{1,2},{2,1},{3,0},{4,7},{5,6},{6,5},{7,4},{8,11},{9,10},{10,... | collective-permute-start | bytes 208904 | tf_op jit(solution)/shard_map/ppermute | solution.py:215
  9.6 4.8 %collective-permute-start = (f32[136,128]{1,0:T(8,128)S(1)}, f32[136,128]{1,0:T(8,128)S(1)}, u32[]{:S(2)}, u32[]{:S(2)}) collective-permute-start(f32[136,128]{1,0:T(8,128)S(1)} %get-tuple-element.45), channel_id=1, source_target_pairs={{0,1},{1,0},{2,3},{3,2},{4,5},{5,4},{6,7},{7,6},{8,9},{9,8},{10,11... | collective-permute-start | bytes 208904 | tf_op jit(solution)/shard_map/ppermute | solution.py:215
  15.2 6.0 %collective-permute-start.3 = (f32[128,128]{1,0:T(8,128)S(1)}, f32[128,128]{1,0:T(8,128)S(1)}, u32[]{:S(2)}, u32[]{:S(2)}) collective-permute-start(f32[128,128]{1,0:T(8,128)S(1)} %get-tuple-element.57), channel_id=1, source_target_pairs={{0,1},{1,0},{2,3},{3,2},{4,5},{5,4},{6,7},{7,6},{8,9},{9,8},{10,11... | collective-permute-start | bytes 196616 | tf_op jit(solution)/shard_map/ppermute | solution.py:215
  15.6 7.0 %collective-permute-start.4 = (f32[128,128]{1,0:T(8,128)S(1)}, f32[128,128]{1,0:T(8,128)S(1)}, u32[]{:S(2)}, u32[]{:S(2)}) collective-permute-start(f32[128,128]{1,0:T(8,128)S(1)} %get-tuple-element.63), channel_id=1, source_target_pairs={{0,3},{1,2},{2,1},{3,0},{4,7},{5,6},{6,5},{7,4},{8,11},{9,10},{10,... | collective-permute-start | bytes 196616 | tf_op jit(solution)/shard_map/ppermute | solution.py:215
  19.0 6.1 %collective-permute-start.5 = (f32[128,128]{1,0:T(8,128)S(1)}, f32[128,128]{1,0:T(8,128)S(1)}, u32[]{:S(2)}, u32[]{:S(2)}) collective-permute-start(f32[128,128]{1,0:T(8,128)S(1)} %get-tuple-element.64), channel_id=1, source_target_pairs={{0,2},{1,3},{2,0},{3,1},{4,6},{5,7},{6,4},{7,5},{8,10},{9,11},{10,... | collective-permute-start | bytes 196616 | tf_op jit(solution)/shard_map/ppermute | solution.py:215
  26.0 1.4 %collective-permute-start.6 = (f32[4,64,128]{2,1,0:T(8,128)S(1)}, f32[4,64,128]{2,1,0:T(8,128)S(1)}, u32[]{:S(2)}, u32[]{:S(2)}) collective-permute-start(f32[4,64,128]{2,1,0:T(8,128)S(1)} %get-tuple-element.66), channel_id=1, source_target_pairs={{0,4},{4,0},{8,12},{12,8},{16,20},{20,16},{24,28},{28,24},{1,5},{5... | collective-permute-start | bytes 393224 | tf_op jit(solution)/shard_map/ppermute | solution.py:215
  27.4 4.9 %collective-permute-start.7 = (f32[64,128]{1,0:T(8,128)S(1)}, f32[64,128]{1,0:T(8,128)S(1)}, u32[]{:S(2)}, u32[]{:S(2)}) collective-permute-start(f32[64,128]{1,0:T(8,128)S(1)} %get-tuple-element.67), channel_id=1, source_target_pairs={{0,24},{4,28},{8,16},{12,20},{16,8},{20,12},{24,0},{28,4},{1,25},{... | collective-permute-start | bytes 98312 | tf_op jit(solution)/shard_map/ppermute | solution.py:215
  29.9 3.9 %collective-permute-start.8 = (f32[64,128]{1,0:T(8,128)S(1)}, f32[64,128]{1,0:T(8,128)S(1)}, u32[]{:S(2)}, u32[]{:S(2)}) collective-permute-start(f32[64,128]{1,0:T(8,128)S(1)} %get-tuple-element.68), channel_id=1, source_target_pairs={{0,16},{4,20},{8,24},{12,28},{16,0},{20,4},{24,8},{28,12},{1,17},{... | collective-permute-start | bytes 98312 | tf_op jit(solution)/shard_map/ppermute | solution.py:215
  30.4 3.9 %collective-permute-start.9 = (f32[64,128]{1,0:T(8,128)S(1)}, f32[64,128]{1,0:T(8,128)S(1)}, u32[]{:S(2)}, u32[]{:S(2)}) collective-permute-start(f32[64,128]{1,0:T(8,128)S(1)} %get-tuple-element.69), channel_id=1, source_target_pairs={{0,8},{4,12},{8,0},{12,4},{16,24},{20,28},{24,16},{28,20},{1,9},{5... | collective-permute-start | bytes 98312 | tf_op jit(solution)/shard_map/ppermute | solution.py:215

commit v3 on v2

--- a/solution.py
+++ b/solution.py
@@ -7,22 +7,22 @@
 from jax.experimental.pallas import tpu as pltpu
 from jax.sharding import PartitionSpec as P
 
+
 F32, BF16 = jnp.float32, jnp.bfloat16
 VMEM = pl.BlockSpec(memory_space=pltpu.VMEM)
 HBM = pl.BlockSpec(memory_space=pltpu.HBM)
-SMEM = pl.BlockSpec(memory_space=pltpu.SMEM)
-
-
-def call(kernel, outs, scalars, hbm, vmem, flops=0, scratch=(), grant=24):
+
+
+def call(kernel, outs, hbm, vmem, flops=0, scratch=(), grant=24):
     return pl.pallas_call(
         kernel,
         out_shape=[jax.ShapeDtypeStruct(s, d) for s, d in outs],
-        in_specs=[SMEM] * len(scalars) + [HBM] * len(hbm) + [VMEM] * len(vmem),
+        in_specs=[HBM] * len(hbm) + [VMEM] * len(vmem),
         out_specs=[VMEM] * len(outs),
         scratch_shapes=scratch,
         compiler_params=pltpu.CompilerParams(vmem_limit_bytes=grant << 20),
         cost_estimate=pl.CostEstimate(flops=flops, bytes_accessed=flops // 256, transcendentals=0),
-    )(*scalars, *[pltpu.with_memory_space_constraint(a, pltpu.HBM) for a in hbm], *vmem)
+    )(*[pltpu.with_memory_space_constraint(a, pltpu.HBM) for a in hbm], *vmem)
 
 
 def split(value):
@@ -48,9 +48,9 @@
     return (covered * through).T, through[-1:] * kept[-1:]
 
 
-def features(k, own, block, columns, passing, first, second, sent, kept):
+def features(k, block, columns, passing, first, second, sent, kept):
     slots, rows, _ = block.shape
-    chunk = own[0] ^ k
+    chunk = lax.axis_index("depth") ^ k
     share = columns[pl.ds(pl.multiple_of(chunk * rows, rows), rows), :]
     total = None
     for s in range(slots):
@@ -67,16 +67,18 @@
     sent[rows:] = jnp.broadcast_to(line, (8, sent.shape[1]))
 
 
-def load_kernel(chunks, rest, own, opacity, counts, samples, first, second, target, *refs):
-    blocks, columns, passing, first_in, second_in, target_in = refs[:6]
-    sent, kept = refs[6 : 6 + len(chunks)], refs[6 + len(chunks) : 6 + 2 * len(chunks)]
-    opacity_in, counts_in, sems = refs[-3:]
-    rows = blocks.shape[2]
-    plain = [(opacity, opacity_in), (counts, counts_in), (first, first_in), (second, second_in), (target, target_in)]
+def load_kernel(chunks, rest, opacity, counts, samples, first, second, target, order, *refs):
+    blocks, columns, passing, first_in, second_in, target_in, nearer = refs[:7]
+    sent, kept = refs[7 : 7 + len(chunks)], refs[7 + len(chunks) : 7 + 2 * len(chunks)]
+    opacity_in, counts_in, order_in, sems = refs[-4:]
+    bricks, _, rows, _ = blocks.shape
+    own = lax.axis_index("depth")
+    plain = [(opacity, opacity_in), (counts, counts_in), (first, first_in), (second, second_in)]
+    plain += [(target, target_in), (order, order_in)]
     small = [pltpu.make_async_copy(a, b, sems.at[i]) for i, (a, b) in enumerate(plain)]
     large = {}
     for k in chunks + rest:
-        start = pl.multiple_of((own[0] ^ k) * rows, rows)
+        start = pl.multiple_of((own ^ k) * rows, rows)
         large[k] = pltpu.make_async_copy(samples.at[:, pl.ds(start, rows), :], blocks.at[k], sems.at[len(plain) + k])
     for copy in small[:3] + [large[k] for k in chunks] + small[3:4] + [large[k] for k in rest] + small[4:]:
         copy.start()
@@ -88,23 +90,31 @@
         large[k].wait()
         if spot == 0:
             small[3].wait()
-        features(k, own, blocks.at[k], columns, passing, first_in, second_in, sent[spot], kept[spot])
+        features(k, blocks.at[k], columns, passing, first_in, second_in, sent[spot], kept[spot])
     for k in rest:
         large[k].wait()
     small[4].wait()
-
-
-def near_kernel(chunks, own, blocks, columns, passing, first, second, *outs):
+    small[5].wait()
+    rank = [order_in[0, own ^ k] for k in range(bricks)]
+    spot = lax.broadcasted_iota(jnp.int32, nearer.shape[1:], 0)
+    for k in range(bricks):
+        line = jnp.zeros(nearer.shape[1:], jnp.int32)
+        for j in range(bricks):
+            line = jnp.where(spot == j, jnp.where(rank[j] < rank[k], 1, 0), line)
+        nearer[k] = line
+
+
+def near_kernel(chunks, blocks, columns, passing, first, second, *outs):
     for spot, k in enumerate(chunks):
         sent, kept = outs[spot], outs[len(chunks) + spot]
-        features(k, own, blocks.at[k], columns, passing, first, second, sent, kept)
-
-
-def prepare_kernel(own, blocks, columns, first, *rest):
+        features(k, blocks.at[k], columns, passing, first, second, sent, kept)
+
+
+def prepare_kernel(blocks, columns, first, *rest):
     count, slots, rows, _ = blocks.shape
     totals, (masked, turned, highs, lows) = rest[:count], rest[count:]
     for k in range(count):
-        start = pl.multiple_of((own[0] ^ k) * rows, rows)
+        start = pl.multiple_of((lax.axis_index("depth") ^ k) * rows, rows)
         share = columns[pl.ds(start, rows), :]
         for s in range(slots):
             block = blocks[k, s]
@@ -114,18 +124,17 @@
         highs[k], lows[k] = split(totals[k][...].T)
 
 
-def owner_kernel(own, ranks, target, *rest):
+def owner_kernel(target, nearer, *rest):
     count = (len(rest) - 1) // 2
     given, pixels, grads = rest[:count], rest[count], rest[count + 1 :]
     rows = target.shape[0]
     lines = [given[k][rows : rows + 1, :rows] for k in range(count)]
-    rank = [ranks[0, own[0] ^ k] for k in range(count)]
     veils = []
     for k in range(count):
         veil = jnp.ones((1, rows), F32)
         for j in range(count):
             if j != k:
-                veil = veil * jnp.where(rank[j] < rank[k], lines[j], 1.0)
+                veil = veil * jnp.where(nearer[k, j : j + 1, :rows] > 0, lines[j], 1.0)
         veils.append(veil)
     while len(veils) % 8:
         veils.append(veils[0])
@@ -141,7 +150,7 @@
 
 
 def backward_terms(chunks, grads, masked, turned, highs, lows, second):
-    inner = outer = None
+    inner, outer = [None, None], None
     for spot, k in enumerate(chunks):
         high, low = split(grads[spot][...])
         rows = high.shape[0]
@@ -155,8 +164,9 @@
         for j in range(0, masked.shape[1], group * rows):
             slope = masked[k, j : j + group * rows] * wide
             part = dot(turned[k, :, j : j + group * rows], slope)
-            inner = part if inner is None else inner + part
-    return inner, outer
+            side = j // (group * rows) % 2
+            inner[side] = part if inner[side] is None else inner[side] + part
+    return inner[0] + inner[1], outer
 
 
 def backward_kernel(chunks, masked, turned, highs, lows, second, *rest):
@@ -169,13 +179,13 @@
     out[...] = value[...]
 
 
-def last_kernel(chunks, place, masked, turned, highs, lows, second, early_in, early_out, *rest):
+def last_kernel(chunks, masked, turned, highs, lows, second, early_in, early_out, *rest):
     grads, (keep, send) = rest[: len(chunks)], rest[-2:]
     inner, outer = backward_terms(chunks, grads, masked, turned, highs, lows, second)
     inner, outer = inner + early_in[...], outer + early_out[...]
     pairs, width = keep.shape[0], keep.shape[2]
     few, many = inner.shape[0] // (2 * pairs), outer.shape[0] // (2 * pairs)
-    even = place[0] % 2 == 0
+    even = lax.axis_index("tile") % 2 == 0
 
     def put(a, at, one, two):
         size = one.shape[0]
@@ -190,8 +200,8 @@
         put(a, at, *[outer[(2 * a + p) * many : (2 * a + p + 1) * many] for p in (0, 1)])
 
 
-def pair_kernel(place, keep, came, *outs):
-    pair = place[0] // 2
+def pair_kernel(keep, came, *outs):
+    pair = lax.axis_index("tile") // 2
     for k, out in enumerate(outs):
         out[...] = keep[pair ^ k] + came[pair ^ k]
 
@@ -219,15 +229,13 @@
     slots, rays, enc = samples.shape
     hid, feat = weight_out.shape
     rows = rays // bricks
-    own = lax.axis_index("depth").astype(jnp.int32)[None]
-    place = lax.axis_index("tile").astype(jnp.int32)[None]
-    far = list(range(bricks - 1, bricks // 2 - 1, -1))
+    far = list(range(bricks // 2, bricks))
     near = list(range(bricks // 2 - 1, -1, -1))
     message, sums = ((rows + 8, feat), F32), ((rows, hid), F32)
     flops = 2 * slots * rows * enc * hid
 
     out = call(
-        functools.partial(load_kernel, far, near),
+        functools.partial(load_kernel, far[:1], far[1:] + near),
         [
             ((bricks, slots, rows, enc), BF16),
             ((rays, slots), F32),
@@ -235,34 +243,38 @@
             (weight_in.shape, BF16),
             (weight_out.shape, BF16),
             (target.shape, F32),
-        ]
-        + [message] * len(far)
-        + [sums] * len(far),
-        [own],
-        [opacity, counts, samples, weight_in, weight_out, target],
+            ((bricks, -(-bricks // 8) * 8, 128), jnp.int32),
+            message,
+            sums,
+        ],
+        [opacity, counts, samples, weight_in, weight_out, target, depth_order],
         [],
-        flops=flops * len(far),
+        flops=flops,
         scratch=[
             pltpu.VMEM(opacity.shape, F32),
             pltpu.VMEM(counts.shape, jnp.int32),
-            pltpu.SemaphoreType.DMA((5 + bricks,)),
+            pltpu.SMEM(depth_order.shape, jnp.int32),
+            pltpu.SemaphoreType.DMA((6 + bricks,)),
         ],
     )
-    blocks, columns, passing, first, second, goal = out[:6]
-    sent = dict(zip(far, out[6 : 6 + len(far)]))
-    totals = dict(zip(far, out[6 + len(far) :]))
-    came = {k: partner(sent[k], "depth", bricks, k) for k in far}
-    out = call(
-        functools.partial(near_kernel, near),
-        [message] * len(near) + [sums] * len(near),
-        [own],
-        [],
-        [blocks, columns, passing, first, second],
-        flops=flops * len(near),
-    )
-    sent.update(zip(near, out[: len(near)]))
-    totals.update(zip(near, out[len(near) :]))
-    came.update({k: partner(sent[k], "depth", bricks, k) if k else sent[k] for k in near})
+    blocks, columns, passing, first, second, goal, nearer = out[:7]
+    sent, totals, came = {far[0]: out[7]}, {far[0]: out[8]}, {}
+
+    def forward(chunks):
+        out = call(
+            functools.partial(near_kernel, chunks),
+            [message] * len(chunks) + [sums] * len(chunks),
+            [],
+            [blocks, columns, passing, first, second],
+            flops=flops * len(chunks),
+        )
+        sent.update(zip(chunks, out[: len(chunks)]))
+        totals.update(zip(chunks, out[len(chunks) :]))
+
+    forward(far[1:])
+    forward(near)
+    for k in far + near:
+        came[k] = partner(sent[k], "depth", bricks, k) if k else sent[k]
     masked, turned, highs, lows = call(
         prepare_kernel,
         [
@@ -271,45 +283,38 @@
             ((bricks, hid, rows), BF16),
             ((bricks, hid, rows), BF16),
         ],
-        [own],
         [],
         [blocks, columns, first] + [totals[k] for k in range(bricks)],
         flops=flops * bricks,
     )
     out = call(
-        owner_kernel,
-        [((rows, feat), F32)] * (bricks + 1),
-        [own, depth_order],
-        [],
-        [goal] + [came[k] for k in range(bricks)],
+        owner_kernel, [((rows, feat), F32)] * (bricks + 1), [], [goal, nearer] + [came[k] for k in range(bricks)]
     )
     slopes = dict(enumerate(out[1:]))
     grads = {k: partner(slopes[k], "depth", bricks, k) if k else slopes[k] for k in far + near}
-    (pixels,) = call(store_kernel, [((rows, feat), F32)], [], [], [out[0]])
+    (pixels,) = call(store_kernel, [((rows, feat), F32)], [], [out[0]])
 
     saved = [masked, turned, highs, lows, second]
     gradients = [((enc, hid), F32), ((hid, feat), F32)]
     before = []
-    for k in reversed(near):
+    turns = [0, far[-1]] + near[:-1] + far[:-1]
+    for k in turns[:-1]:
         before = call(
-            functools.partial(backward_kernel, [k]), gradients, [], [], saved + [grads[k]] + list(before), flops=flops
+            functools.partial(backward_kernel, [k]), gradients, [], saved + [grads[k]] + list(before), flops=flops
         )
     pairs = tiles // 2
     part = (enc * hid + hid * feat) // (tiles * feat)
     keep, send = call(
-        functools.partial(last_kernel, far),
+        functools.partial(last_kernel, turns[-1:]),
         [((pairs, part, feat), F32)] * 2,
-        [place],
         [],
-        saved + list(before) + [grads[k] for k in far],
-        flops=flops * len(far),
+        saved + list(before) + [grads[turns[-1]]],
+        flops=flops,
     )
     other = partner(send, "tile", tiles, 1)
-    parts = call(pair_kernel, [((part, feat), F32)] * pairs, [place], [], [keep, other])
+    parts = call(pair_kernel, [((part, feat), F32)] * pairs, [], [keep, other])
     parts = [partner(parts[k], "tile", tiles, 2 * k) if k else parts[k] for k in range(pairs - 1, -1, -1)]
-    grad_in, grad_out = call(
-        finish_kernel, [((1, enc // tiles, hid), F32), ((1, hid // tiles, feat), F32)], [], [], parts
-    )
+    grad_in, grad_out = call(finish_kernel, [((1, enc // tiles, hid), F32), ((1, hid // tiles, feat), F32)], [], parts)
     return pixels, grad_in, grad_out
 
 

time: 35.1 us -> 32.6 us (0.929)
  waiting for transfers between devices: 11.8 us -> 8.9 us
  starting transfers between devices: 13.1 us -> 13.9 us
  Pallas kernels: 9.33 us -> 8.91 us
    ppermute x10, waiting for transfers between devices: 11.8 us -> 8.9 us  [partner(): return lax.ppermute(value, axis, [(i, i ^ k) for i in range(size)])]
    ppermute x10, starting transfers between devices: 13.1 us -> 13.9 us  [partner(): return lax.ppermute(value, axis, [(i, i ^ k) for i in range(size)])]
    pallas_call x10 -> x12, Pallas kernels: 9.33 us -> 8.91 us  [call(): pl.pallas_call(kernel, out_shape=[jax.ShapeDtypeStruct(s, d) for s, d in...]
  transfers between devices with their start and end apart: 10 -> 10, of which waited for: 9 -> 9; matrix products, arithmetic and copies ran while one was open for 0% -> 0% of each run, Pallas kernels for 13% -> 17%
where the time goes in v3:
time: 32.6 us; the launch traced here: 32.4 us
  starting transfers between devices  13.9 us (43%)
  Pallas kernels  8.91 us (27%)
  waiting for transfers between devices  8.9 us (27%)
  between operations  0.72 us (2%)
    ppermute x10, starting transfers between devices, partner(): return lax.ppermute(value, axis, [(i, i ^ k) for i in range(size)])  13.9 us
    pallas_call x12, Pallas kernels, call(): pl.pallas_call(kernel, out_shape=[jax.ShapeDtypeStruct(s, d) for s, d in...  8.91 us
    ppermute x10, waiting for transfers between devices, partner(): return lax.ppermute(value, axis, [(i, i ^ k) for i in range(size)])  8.9 us
  transfers between devices with their start and end apart: 10, of which 9 were waited for; matrix products, arithmetic and copies ran while one was open for 0% of the time, Pallas kernels for 17%

profile of v3, /device:TPU:0, one launch (start us, length us, event | category | flops | bytes accessed | tf_op | source)
XLA Modules:
  0.0 32.4 jit_solution(2844519704148123567)
XLA Ops:
  0.6 1.8 %shard_map.94 = (bf16[4,16,128,128]{3,2,1,0:T(8,128)(2,1)S(1)}, f32[512,16]{1,0:T(8,128)S(1)}, f32[1,512]{1,0:T(1,128)S(1)}, bf16[128,256]{1,0:T(8,128)(2,1)S(1)...) custom-call(f32[16,512]{1,0:T(8,128)} %bitcast.7, ...), custom_call_target="tpu_custom_call" | custom-call | flops 134217728 | bytes 524288 | tf_op jit(solution)/shard_map/pallas_call | solution.py:17
  2.5 4.1 %collective-permute-start.1 = (f32[136,128]{1,0:T(8,128)S(1)}, f32[136,128]{1,0:T(8,128)S(1)}, u32[]{:S(2)}, u32[]{:S(2)}) collective-permute-start(f32[136,128]{1,0:T(8,128)S(1)} %get-tuple-element.50), channel_id=1, source_target_pairs={{0,2},{1,3},{2,0},{3,1},{4,6},{5,7},{6,4},{7,5},{8,10},{9,11},{10,... | collective-permute-start | bytes 208904 | tf_op jit(solution)/shard_map/ppermute | solution.py:225
  6.6 0.6 %shard_map.96 = (f32[136,128]{1,0:T(8,128)S(1)}, f32[128,256]{1,0:T(8,128)S(1)}) custom-call(bf16[4,16,128,128]{3,2,1,0:T(8,128)(2,1)S(1)} %get-tuple-element.43.blocks, f32[512,16]{1,0:T(8,128)S(1)} %get-tuple-element.44.columns, f32[1,512]{1,0:T(1,128)S(1)} %get-tuple-element.45.passing, bf16[128,256]{1,0:T(8,128)(2,1)S(1)} %get-tuple-element.46.first, ...), custom_call_target="tpu_custom_call" | custom-call | flops 134217728 | bytes 524288 | tf_op jit(solution)/shard_map/pallas_call | solution.py:17
  7.2 1.4 %collective-permute-start.2 = (f32[136,128]{1,0:T(8,128)S(1)}, f32[136,128]{1,0:T(8,128)S(1)}, u32[]{:S(2)}, u32[]{:S(2)}) collective-permute-start(f32[136,128]{1,0:T(8,128)S(1)} %get-tuple-element.51), channel_id=1, source_target_pairs={{0,3},{1,2},{2,1},{3,0},{4,7},{5,6},{6,5},{7,4},{8,11},{9,10},{10,... | collective-permute-start | bytes 208904 | tf_op jit(solution)/shard_map/ppermute | solution.py:225
  8.6 1.0 %shard_map.95 = (f32[136,128]{1,0:T(8,128)S(1)}, f32[136,128]{1,0:T(8,128)S(1)}, f32[128,256]{1,0:T(8,128)S(1)}, f32[128,256]{1,0:T(8,128)S(1)}) custom-call(bf16[4,16,128,128]{3,2,1,0:T(8,128)(2,1)S(1)} %get-tuple-element.43.blocks, f32[512,16]{1,0:T(8,128)S(1)} %get-tuple-element.44.columns, f32[1,512]{1,0:T(1,128)S(1)} %get-tuple-element.45.passing, ...), custom_call_target="tpu_custom_call" | custom-call | flops 268435456 | bytes 1048576 | tf_op jit(solution)/shard_map/pallas_call | solution.py:17
  9.6 0.3 collective-permute-start
  9.9 0.5 %collective-permute-done.1.rest_2_ = f32[136,128]{1,0:T(8,128)S(1)} collective-permute-done((f32[136,128]{1,0:T(8,128)S(1)}, f32[136,128]{1,0:T(8,128)S(1)}, u32[]{:S(2)}, u32[]{:S(2)}) %collective-permute-start.1) | collective-permute-done | bytes 69664 | tf_op jit(solution)/shard_map/ppermute | solution.py:225
  10.4 3.7 %collective-permute-done.2.rest_3_ = f32[136,128]{1,0:T(8,128)S(1)} collective-permute-done((f32[136,128]{1,0:T(8,128)S(1)}, f32[136,128]{1,0:T(8,128)S(1)}, u32[]{:S(2)}, u32[]{:S(2)}) %collective-permute-start.2) | collective-permute-done | bytes 69664 | tf_op jit(solution)/shard_map/ppermute | solution.py:225
  14.0 0.3 %collective-permute-done.rest_1_ = f32[136,128]{1,0:T(8,128)S(1)} collective-permute-done((f32[136,128]{1,0:T(8,128)S(1)}, f32[136,128]{1,0:T(8,128)S(1)}, u32[]{:S(2)}, u32[]{:S(2)}) %collective-permute-start) | collective-permute-done | bytes 69664 | tf_op jit(solution)/shard_map/ppermute | solution.py:225
  14.4 0.3 shard_map.97
  14.6 2.5 %collective-permute-start.4 = (f32[128,128]{1,0:T(8,128)S(1)}, f32[128,128]{1,0:T(8,128)S(1)}, u32[]{:S(2)}, u32[]{:S(2)}) collective-permute-start(f32[128,128]{1,0:T(8,128)S(1)} %get-tuple-element.62), channel_id=1, source_target_pairs={{0,3},{1,2},{2,1},{3,0},{4,7},{5,6},{6,5},{7,4},{8,11},{9,10},{10,... | collective-permute-start | bytes 196616 | tf_op jit(solution)/shard_map/ppermute | solution.py:225
  17.1 0.0 collective-permute-start.3
  17.1 2.0 %collective-permute-start.5 = (f32[128,128]{1,0:T(8,128)S(1)}, f32[128,128]{1,0:T(8,128)S(1)}, u32[]{:S(2)}, u32[]{:S(2)}) collective-permute-start(f32[128,128]{1,0:T(8,128)S(1)} %get-tuple-element.70), channel_id=1, source_target_pairs={{0,2},{1,3},{2,0},{3,1},{4,6},{5,7},{6,4},{7,5},{8,10},{9,11},{10,... | collective-permute-start | bytes 196616 | tf_op jit(solution)/shard_map/ppermute | solution.py:225
  19.1 1.7 %shard_map.99 = (bf16[4,2048,256]{2,1,0:T(8,128)(2,1)S(1)}, bf16[4,128,2048]{2,1,0:T(8,128)(2,1)S(1)}, bf16[4,256,128]{2,1,0:T(8,128)(2,1)S(1)}, bf16[4,256,128]{2,1,0:T(8,128)(2,1)S(1)}) custom-call(bf16[4,16,128,128]{3,2,1,0:T(8,128)(2,1)S(1)} %get-tuple-element.43.blocks, f32[512,16]{1,0:T(8,128)S(1)} %get-tuple-element.44.columns, ...), custom_call_target="tpu_custom_call" | custom-call | flops 536870912 | bytes 2097152 | tf_op jit(solution)/shard_map/pallas_call | solution.py:17
  20.8 0.6 %shard_map.100 = (f32[128,256]{1,0:T(8,128)S(1)}, f32[256,128]{1,0:T(8,128)S(1)}) custom-call(bf16[4,2048,256]{2,1,0:T(8,128)(2,1)S(1)} %get-tuple-element.57.masked, bf16[4,128,2048]{2,1,0:T(8,128)(2,1)S(1)} %get-tuple-element.58.turned, bf16[4,256,128]{2,1,0:T(8,128)(2,1)S(1)} %get-tuple-element.59.highs, bf16[4,256,128]{2,1,0:T(8,128)(2,1)S(1)} %get-tuple-element.60.lows, ...), custom_call_target="tpu_custom_call" | custom-call | flops 134217728 | bytes 524288 | tf_op jit(solution)/shard_map/pallas_call | solution.py:17
  21.3 0.0 collective-permute-done.4.rest_0_
  21.4 0.6 %shard_map.101 = (f32[128,256]{1,0:T(8,128)S(1)}, f32[256,128]{1,0:T(8,128)S(1)}) custom-call(bf16[4,2048,256]{2,1,0:T(8,128)(2,1)S(1)} %get-tuple-element.57.masked, bf16[4,128,2048]{2,1,0:T(8,128)(2,1)S(1)} %get-tuple-element.58.turned, bf16[4,256,128]{2,1,0:T(8,128)(2,1)S(1)} %get-tuple-element.59.highs, bf16[4,256,128]{2,1,0:T(8,128)(2,1)S(1)} %get-tuple-element.60.lows, ...), custom_call_target="tpu_custom_call" | custom-call | flops 134217728 | bytes 524288 | tf_op jit(solution)/shard_map/pallas_call | solution.py:17
  21.9 0.2 collective-permute-done.3.rest_0_
  22.2 0.6 %shard_map.102 = (f32[128,256]{1,0:T(8,128)S(1)}, f32[256,128]{1,0:T(8,128)S(1)}) custom-call(bf16[4,2048,256]{2,1,0:T(8,128)(2,1)S(1)} %get-tuple-element.57.masked, bf16[4,128,2048]{2,1,0:T(8,128)(2,1)S(1)} %get-tuple-element.58.turned, bf16[4,256,128]{2,1,0:T(8,128)(2,1)S(1)} %get-tuple-element.59.highs, bf16[4,256,128]{2,1,0:T(8,128)(2,1)S(1)} %get-tuple-element.60.lows, ...), custom_call_target="tpu_custom_call" | custom-call | flops 134217728 | bytes 524288 | tf_op jit(solution)/shard_map/pallas_call | solution.py:17
  22.8 0.1 collective-permute-done.5.rest_0_
  22.9 0.6 %shard_map.103 = (f32[4,64,128]{2,1,0:T(8,128)S(1)}, f32[4,64,128]{2,1,0:T(8,128)S(1)}) custom-call(bf16[4,2048,256]{2,1,0:T(8,128)(2,1)S(1)} %get-tuple-element.57.masked, bf16[4,128,2048]{2,1,0:T(8,128)(2,1)S(1)} %get-tuple-element.58.turned, bf16[4,256,128]{2,1,0:T(8,128)(2,1)S(1)} %get-tuple-element.59.highs, ...), custom_call_target="tpu_custom_call" | custom-call | flops 134217728 | bytes 524288 | tf_op jit(solution)/shard_map/pallas_call | solution.py:17
  23.4 0.1 collective-permute-start.6
  23.5 1.3 %collective-permute-done.6.came = f32[4,64,128]{2,1,0:T(8,128)S(1)} collective-permute-done((f32[4,64,128]{2,1,0:T(8,128)S(1)}, f32[4,64,128]{2,1,0:T(8,128)S(1)}, u32[]{:S(2)}, u32[]{:S(2)}) %collective-permute-start.6) | collective-permute-done | bytes 131104 | tf_op jit(solution)/shard_map/ppermute | solution.py:225
  24.9 2.5 %collective-permute-start.7 = (f32[64,128]{1,0:T(8,128)S(1)}, f32[64,128]{1,0:T(8,128)S(1)}, u32[]{:S(2)}, u32[]{:S(2)}) collective-permute-start(f32[64,128]{1,0:T(8,128)S(1)} %get-tuple-element.73), channel_id=1, source_target_pairs={{0,24},{4,28},{8,16},{12,20},{16,8},{20,12},{24,0},{28,4},{1,25},{... | collective-permute-start | bytes 98312 | tf_op jit(solution)/shard_map/ppermute | solution.py:225
  27.4 0.5 %collective-permute-start.8 = (f32[64,128]{1,0:T(8,128)S(1)}, f32[64,128]{1,0:T(8,128)S(1)}, u32[]{:S(2)}, u32[]{:S(2)}) collective-permute-start(f32[64,128]{1,0:T(8,128)S(1)} %get-tuple-element.74), channel_id=1, source_target_pairs={{0,16},{4,20},{8,24},{12,28},{16,0},{20,4},{24,8},{28,12},{1,17},{... | collective-permute-start | bytes 98312 | tf_op jit(solution)/shard_map/ppermute | solution.py:225
  27.9 0.5 %collective-permute-start.9 = (f32[64,128]{1,0:T(8,128)S(1)}, f32[64,128]{1,0:T(8,128)S(1)}, u32[]{:S(2)}, u32[]{:S(2)}) collective-permute-start(f32[64,128]{1,0:T(8,128)S(1)} %get-tuple-element.75), channel_id=1, source_target_pairs={{0,8},{4,12},{8,0},{12,4},{16,24},{20,28},{24,16},{28,20},{1,9},{5... | collective-permute-start | bytes 98312 | tf_op jit(solution)/shard_map/ppermute | solution.py:225
  28.4 0.6 %shard_map.98 = f32[128,128]{1,0:T(8,128)} custom-call(f32[128,128]{1,0:T(8,128)S(1)} %get-tuple-element.52.value), custom_call_target="tpu_custom_call" | custom-call | tf_op jit(solution)/shard_map/pallas_call | solution.py:17
  29.1 0.7 %collective-permute-done.7.refs_0_ = f32[64,128]{1,0:T(8,128)S(1)} collective-permute-done((f32[64,128]{1,0:T(8,128)S(1)}, f32[64,128]{1,0:T(8,128)S(1)}, u32[]{:S(2)}, u32[]{:S(2)}) %collective-permute-start.7) | collective-permute-done | bytes 32800 | tf_op jit(solution)/shard_map/ppermute | solution.py:225
  29.7 1.6 %collective-permute-done.8.refs_1_ = f32[64,128]{1,0:T(8,128)S(1)} collective-permute-done((f32[64,128]{1,0:T(8,128)S(1)}, f32[64,128]{1,0:T(8,128)S(1)}, u32[]{:S(2)}, u32[]{:S(2)}) %collective-permute-start.8) | collective-permute-done | bytes 32800 | tf_op jit(solution)/shard_map/ppermute | solution.py:225
  31.3 0.5 %collective-permute-done.9.refs_2_ = f32[64,128]{1,0:T(8,128)S(1)} collective-permute-done((f32[64,128]{1,0:T(8,128)S(1)}, f32[64,128]{1,0:T(8,128)S(1)}, u32[]{:S(2)}, u32[]{:S(2)}) %collective-permute-start.9) | collective-permute-done | bytes 32800 | tf_op jit(solution)/shard_map/ppermute | solution.py:225
  31.8 0.6 %shard_map.105 = (f32[1,16,256]{2,1,0:T(8,128)}, f32[1,32,128]{2,1,0:T(8,128)}) custom-call(f32[64,128]{1,0:T(8,128)S(1)} %collective-permute-done.7.refs_0_, f32[64,128]{1,0:T(8,128)S(1)} %collective-permute-done.8.refs_1_, f32[64,128]{1,0:T(8,128)S(1)} %collective-permute-done.9.refs_2_, f32[64,128]{1,0:T(8,128)S(1)} %get-tuple-element.76.refs_3_), custom_call_target="tpu_custom_call" | custom-call | tf_op jit(solution)/shard_map/pallas_call | solution.py:17
  (1 shorter events, 0.0 us)
Async XLA Ops:
  2.5 7.9 %collective-permute-start.1 = (f32[136,128]{1,0:T(8,128)S(1)}, f32[136,128]{1,0:T(8,128)S(1)}, u32[]{:S(2)}, u32[]{:S(2)}) collective-permute-start(f32[136,128]{1,0:T(8,128)S(1)} %get-tuple-element.50), channel_id=1, source_target_pairs={{0,2},{1,3},{2,0},{3,1},{4,6},{5,7},{6,4},{7,5},{8,10},{9,11},{10,... | collective-permute-start | bytes 208904 | tf_op jit(solution)/shard_map/ppermute | solution.py:225
  7.2 6.9 %collective-permute-start.2 = (f32[136,128]{1,0:T(8,128)S(1)}, f32[136,128]{1,0:T(8,128)S(1)}, u32[]{:S(2)}, u32[]{:S(2)}) collective-permute-start(f32[136,128]{1,0:T(8,128)S(1)} %get-tuple-element.51), channel_id=1, source_target_pairs={{0,3},{1,2},{2,1},{3,0},{4,7},{5,6},{6,5},{7,4},{8,11},{9,10},{10,... | collective-permute-start | bytes 208904 | tf_op jit(solution)/shard_map/ppermute | solution.py:225
  9.6 4.8 %collective-permute-start = (f32[136,128]{1,0:T(8,128)S(1)}, f32[136,128]{1,0:T(8,128)S(1)}, u32[]{:S(2)}, u32[]{:S(2)}) collective-permute-start(f32[136,128]{1,0:T(8,128)S(1)} %get-tuple-element.49), channel_id=1, source_target_pairs={{0,1},{1,0},{2,3},{3,2},{4,5},{5,4},{6,7},{7,6},{8,9},{9,8},{10,11... | collective-permute-start | bytes 208904 | tf_op jit(solution)/shard_map/ppermute | solution.py:225
  14.6 6.7 %collective-permute-start.4 = (f32[128,128]{1,0:T(8,128)S(1)}, f32[128,128]{1,0:T(8,128)S(1)}, u32[]{:S(2)}, u32[]{:S(2)}) collective-permute-start(f32[128,128]{1,0:T(8,128)S(1)} %get-tuple-element.62), channel_id=1, source_target_pairs={{0,3},{1,2},{2,1},{3,0},{4,7},{5,6},{6,5},{7,4},{8,11},{9,10},{10,... | collective-permute-start | bytes 196616 | tf_op jit(solution)/shard_map/ppermute | solution.py:225
  17.1 5.1 %collective-permute-start.3 = (f32[128,128]{1,0:T(8,128)S(1)}, f32[128,128]{1,0:T(8,128)S(1)}, u32[]{:S(2)}, u32[]{:S(2)}) collective-permute-start(f32[128,128]{1,0:T(8,128)S(1)} %get-tuple-element.61), channel_id=1, source_target_pairs={{0,1},{1,0},{2,3},{3,2},{4,5},{5,4},{6,7},{7,6},{8,9},{9,8},{10,11... | collective-permute-start | bytes 196616 | tf_op jit(solution)/shard_map/ppermute | solution.py:225
  17.1 5.7 %collective-permute-start.5 = (f32[128,128]{1,0:T(8,128)S(1)}, f32[128,128]{1,0:T(8,128)S(1)}, u32[]{:S(2)}, u32[]{:S(2)}) collective-permute-start(f32[128,128]{1,0:T(8,128)S(1)} %get-tuple-element.70), channel_id=1, source_target_pairs={{0,2},{1,3},{2,0},{3,1},{4,6},{5,7},{6,4},{7,5},{8,10},{9,11},{10,... | collective-permute-start | bytes 196616 | tf_op jit(solution)/shard_map/ppermute | solution.py:225
  23.4 1.4 %collective-permute-start.6 = (f32[4,64,128]{2,1,0:T(8,128)S(1)}, f32[4,64,128]{2,1,0:T(8,128)S(1)}, u32[]{:S(2)}, u32[]{:S(2)}) collective-permute-start(f32[4,64,128]{2,1,0:T(8,128)S(1)} %get-tuple-element.72), channel_id=1, source_target_pairs={{0,4},{4,0},{8,12},{12,8},{16,20},{20,16},{24,28},{28,24},{1,5},{5... | collective-permute-start | bytes 393224 | tf_op jit(solution)/shard_map/ppermute | solution.py:225
  24.9 4.9 %collective-permute-start.7 = (f32[64,128]{1,0:T(8,128)S(1)}, f32[64,128]{1,0:T(8,128)S(1)}, u32[]{:S(2)}, u32[]{:S(2)}) collective-permute-start(f32[64,128]{1,0:T(8,128)S(1)} %get-tuple-element.73), channel_id=1, source_target_pairs={{0,24},{4,28},{8,16},{12,20},{16,8},{20,12},{24,0},{28,4},{1,25},{... | collective-permute-start | bytes 98312 | tf_op jit(solution)/shard_map/ppermute | solution.py:225
  27.4 3.9 %collective-permute-start.8 = (f32[64,128]{1,0:T(8,128)S(1)}, f32[64,128]{1,0:T(8,128)S(1)}, u32[]{:S(2)}, u32[]{:S(2)}) collective-permute-start(f32[64,128]{1,0:T(8,128)S(1)} %get-tuple-element.74), channel_id=1, source_target_pairs={{0,16},{4,20},{8,24},{12,28},{16,0},{20,4},{24,8},{28,12},{1,17},{... | collective-permute-start | bytes 98312 | tf_op jit(solution)/shard_map/ppermute | solution.py:225
  27.9 3.9 %collective-permute-start.9 = (f32[64,128]{1,0:T(8,128)S(1)}, f32[64,128]{1,0:T(8,128)S(1)}, u32[]{:S(2)}, u32[]{:S(2)}) collective-permute-start(f32[64,128]{1,0:T(8,128)S(1)} %get-tuple-element.75), channel_id=1, source_target_pairs={{0,8},{4,12},{8,0},{12,4},{16,24},{20,28},{24,16},{28,20},{1,9},{5... | collective-permute-start | bytes 98312 | tf_op jit(solution)/shard_map/ppermute | solution.py:225

commit v4 on v3

--- a/solution.py
+++ b/solution.py
@@ -58,13 +58,13 @@
         total = term if total is None else total + term
     kept[...] = total
     high, low = split(total)
-    sent[:rows] = dot(high, second[...]) + dot(low, second[...])
+    sent[:rows, 0] = dot(high, second[...]) + dot(low, second[...])
     line = jnp.zeros((1, rows), F32)
     for c in range(passing.shape[1] // rows):
         line = jnp.where(chunk == c, passing[:, c * rows : (c + 1) * rows], line)
-    if rows < sent.shape[1]:
-        line = jnp.concatenate([line, jnp.zeros((1, sent.shape[1] - rows), F32)], axis=1)
-    sent[rows:] = jnp.broadcast_to(line, (8, sent.shape[1]))
+    if rows < sent.shape[2]:
+        line = jnp.concatenate([line, jnp.zeros((1, sent.shape[2] - rows), F32)], axis=1)
+    sent[rows] = line
 
 
 def load_kernel(chunks, rest, opacity, counts, samples, first, second, target, order, *refs):
@@ -128,7 +128,7 @@
     count = (len(rest) - 1) // 2
     given, pixels, grads = rest[:count], rest[count], rest[count + 1 :]
     rows = target.shape[0]
-    lines = [given[k][rows : rows + 1, :rows] for k in range(count)]
+    lines = [given[k][rows][:, :rows] for k in range(count)]
     veils = []
     for k in range(count):
         veil = jnp.ones((1, rows), F32)
@@ -141,7 +141,7 @@
     turned = jnp.concatenate(veils, axis=0).T
     total = None
     for k in range(count):
-        term = given[k][:rows] * turned[:, k : k + 1]
+        term = given[k][:rows, 0] * turned[:, k : k + 1]
         total = term if total is None else total + term
     pixels[...] = total
     slope = total - target[...]
@@ -155,8 +155,8 @@
         high, low = split(grads[spot][...])
         rows = high.shape[0]
         across = (((1,), (1,)), ((), ()))
-        back = lax.dot_general(high, second[...], across, preferred_element_type=F32)
-        back = (back + lax.dot_general(low, second[...], across, preferred_element_type=F32)).astype(BF16)
+        both, twice = jnp.concatenate([high, low], axis=1), jnp.concatenate([second[...]] * 2, axis=1)
+        back = lax.dot_general(both, twice, across, preferred_element_type=F32).astype(BF16)
         part = dot(highs[k], high) + dot(highs[k], low) + dot(lows[k], high)
         outer = part if outer is None else outer + part
         group = 2
@@ -231,7 +231,7 @@
     rows = rays // bricks
     far = list(range(bricks // 2, bricks))
     near = list(range(bricks // 2 - 1, -1, -1))
-    message, sums = ((rows + 8, feat), F32), ((rows, hid), F32)
+    message, sums = ((rows + 1, 1, feat), F32), ((rows, hid), F32)
     flops = 2 * slots * rows * enc * hid
 
     out = call(

time: 32.6 us -> 32.3 us (level)
  waiting for transfers between devices: 8.9 us -> 8.54 us
    ppermute x10, waiting for transfers between devices: 8.9 us -> 8.54 us  [partner(): return lax.ppermute(value, axis, [(i, i ^ k) for i in range(size)])]
  transfers between devices with their start and end apart: 10 -> 10, of which waited for: 9 -> 8; matrix products, arithmetic and copies ran while one was open for 0% -> 0% of each run, Pallas kernels for 17% -> 18%
where the time goes in v4:
time: 32.3 us; the launch traced here: 32.2 us
  starting transfers between devices  13.9 us (43%)
  Pallas kernels  8.96 us (28%)
  waiting for transfers between devices  8.54 us (26%)
  between operations  0.73 us (2%)
    ppermute x10, starting transfers between devices, partner(): return lax.ppermute(value, axis, [(i, i ^ k) for i in range(size)])  13.9 us
    pallas_call x12, Pallas kernels, call(): pl.pallas_call(kernel, out_shape=[jax.ShapeDtypeStruct(s, d) for s, d in...  8.96 us
    ppermute x10, waiting for transfers between devices, partner(): return lax.ppermute(value, axis, [(i, i ^ k) for i in range(size)])  8.54 us
  transfers between devices with their start and end apart: 10, of which 8 were waited for; matrix products, arithmetic and copies ran while one was open for 0% of the time, Pallas kernels for 18%

profile of v4, /device:TPU:0, one launch (start us, length us, event | category | flops | bytes accessed | tf_op | source)
XLA Modules:
  0.0 32.2 jit_solution(12505770831945501596)
XLA Ops:
  0.6 1.8 %shard_map.94 = (bf16[4,16,128,128]{3,2,1,0:T(8,128)(2,1)S(1)}, f32[512,16]{1,0:T(8,128)S(1)}, f32[1,512]{1,0:T(1,128)S(1)}, bf16[128,256]{1,0:T(8,128)(2,1)S(1)...) custom-call(f32[16,512]{1,0:T(8,128)} %bitcast.7, ...), custom_call_target="tpu_custom_call" | custom-call | flops 134217728 | bytes 524288 | tf_op jit(solution)/shard_map/pallas_call | solution.py:17
  2.5 4.1 %collective-permute-start.1 = (f32[129,1,128]{2,1,0:T(1,128)S(1)}, f32[129,1,128]{2,1,0:T(1,128)S(1)}, u32[]{:S(2)}, u32[]{:S(2)}) collective-permute-start(f32[129,1,128]{2,1,0:T(1,128)S(1)} %get-tuple-element.50), channel_id=1, source_target_pairs={{0,2},{1,3},{2,0},{3,1},{4,6},{5,7},{6,4},{7,5},{8,10},{9,11},{10,... | collective-permute-start | bytes 198152 | tf_op jit(solution)/shard_map/ppermute | solution.py:225
  6.6 0.6 %shard_map.96 = (f32[129,1,128]{2,1,0:T(1,128)S(1)}, f32[128,256]{1,0:T(8,128)S(1)}) custom-call(bf16[4,16,128,128]{3,2,1,0:T(8,128)(2,1)S(1)} %get-tuple-element.43.blocks, f32[512,16]{1,0:T(8,128)S(1)} %get-tuple-element.44.columns, f32[1,512]{1,0:T(1,128)S(1)} %get-tuple-element.45.passing, bf16[128,256]{1,0:T(8,128)(2,1)S(1)} %get-tuple-element.46.first, ...), custom_call_target="tpu_custom_call" | custom-call | flops 134217728 | bytes 524288 | tf_op jit(solution)/shard_map/pallas_call | solution.py:17
  7.2 1.4 %collective-permute-start.2 = (f32[129,1,128]{2,1,0:T(1,128)S(1)}, f32[129,1,128]{2,1,0:T(1,128)S(1)}, u32[]{:S(2)}, u32[]{:S(2)}) collective-permute-start(f32[129,1,128]{2,1,0:T(1,128)S(1)} %get-tuple-element.51), channel_id=1, source_target_pairs={{0,3},{1,2},{2,1},{3,0},{4,7},{5,6},{6,5},{7,4},{8,11},{9,10},{10,... | collective-permute-start | bytes 198152 | tf_op jit(solution)/shard_map/ppermute | solution.py:225
  8.6 1.0 %shard_map.95 = (f32[129,1,128]{2,1,0:T(1,128)S(1)}, f32[129,1,128]{2,1,0:T(1,128)S(1)}, f32[128,256]{1,0:T(8,128)S(1)}, f32[128,256]{1,0:T(8,128)S(1)}) custom-call(bf16[4,16,128,128]{3,2,1,0:T(8,128)(2,1)S(1)} %get-tuple-element.43.blocks, f32[512,16]{1,0:T(8,128)S(1)} %get-tuple-element.44.columns, f32[1,512]{1,0:T(1,128)S(1)} %get-tuple-element.45.passing, ...), custom_call_target="tpu_custom_call" | custom-call | flops 268435456 | bytes 1048576 | tf_op jit(solution)/shard_map/pallas_call | solution.py:17
  9.6 0.3 collective-permute-start
  10.0 0.3 collective-permute-done.1.rest_2_
  10.3 3.7 %collective-permute-done.2.rest_3_ = f32[129,1,128]{2,1,0:T(1,128)S(1)} collective-permute-done((f32[129,1,128]{2,1,0:T(1,128)S(1)}, f32[129,1,128]{2,1,0:T(1,128)S(1)}, u32[]{:S(2)}, u32[]{:S(2)}) %collective-permute-start.2) | collective-permute-done | bytes 66080 | tf_op jit(solution)/shard_map/ppermute | solution.py:225
  14.0 0.4 %collective-permute-done.rest_1_ = f32[129,1,128]{2,1,0:T(1,128)S(1)} collective-permute-done((f32[129,1,128]{2,1,0:T(1,128)S(1)}, f32[129,1,128]{2,1,0:T(1,128)S(1)}, u32[]{:S(2)}, u32[]{:S(2)}) %collective-permute-start) | collective-permute-done | bytes 66080 | tf_op jit(solution)/shard_map/ppermute | solution.py:225
  14.3 0.3 shard_map.97
  14.6 2.3 %collective-permute-start.4 = (f32[128,128]{1,0:T(8,128)S(1)}, f32[128,128]{1,0:T(8,128)S(1)}, u32[]{:S(2)}, u32[]{:S(2)}) collective-permute-start(f32[128,128]{1,0:T(8,128)S(1)} %get-tuple-element.62), channel_id=1, source_target_pairs={{0,3},{1,2},{2,1},{3,0},{4,7},{5,6},{6,5},{7,4},{8,11},{9,10},{10,... | collective-permute-start | bytes 196616 | tf_op jit(solution)/shard_map/ppermute | solution.py:225
  16.9 0.0 collective-permute-start.3
  16.9 2.2 %collective-permute-start.5 = (f32[128,128]{1,0:T(8,128)S(1)}, f32[128,128]{1,0:T(8,128)S(1)}, u32[]{:S(2)}, u32[]{:S(2)}) collective-permute-start(f32[128,128]{1,0:T(8,128)S(1)} %get-tuple-element.70), channel_id=1, source_target_pairs={{0,2},{1,3},{2,0},{3,1},{4,6},{5,7},{6,4},{7,5},{8,10},{9,11},{10,... | collective-permute-start | bytes 196616 | tf_op jit(solution)/shard_map/ppermute | solution.py:225
  19.1 1.7 %shard_map.99 = (bf16[4,2048,256]{2,1,0:T(8,128)(2,1)S(1)}, bf16[4,128,2048]{2,1,0:T(8,128)(2,1)S(1)}, bf16[4,256,128]{2,1,0:T(8,128)(2,1)S(1)}, bf16[4,256,128]{2,1,0:T(8,128)(2,1)S(1)}) custom-call(bf16[4,16,128,128]{3,2,1,0:T(8,128)(2,1)S(1)} %get-tuple-element.43.blocks, f32[512,16]{1,0:T(8,128)S(1)} %get-tuple-element.44.columns, ...), custom_call_target="tpu_custom_call" | custom-call | flops 536870912 | bytes 2097152 | tf_op jit(solution)/shard_map/pallas_call | solution.py:17
  20.7 0.6 %shard_map.100 = (f32[128,256]{1,0:T(8,128)S(1)}, f32[256,128]{1,0:T(8,128)S(1)}) custom-call(bf16[4,2048,256]{2,1,0:T(8,128)(2,1)S(1)} %get-tuple-element.57.masked, bf16[4,128,2048]{2,1,0:T(8,128)(2,1)S(1)} %get-tuple-element.58.turned, bf16[4,256,128]{2,1,0:T(8,128)(2,1)S(1)} %get-tuple-element.59.highs, bf16[4,256,128]{2,1,0:T(8,128)(2,1)S(1)} %get-tuple-element.60.lows, ...), custom_call_target="tpu_custom_call" | custom-call | flops 134217728 | bytes 524288 | tf_op jit(solution)/shard_map/pallas_call | solution.py:17
  21.3 0.0 collective-permute-done.4.rest_0_
  21.3 0.6 %shard_map.101 = (f32[128,256]{1,0:T(8,128)S(1)}, f32[256,128]{1,0:T(8,128)S(1)}) custom-call(bf16[4,2048,256]{2,1,0:T(8,128)(2,1)S(1)} %get-tuple-element.57.masked, bf16[4,128,2048]{2,1,0:T(8,128)(2,1)S(1)} %get-tuple-element.58.turned, bf16[4,256,128]{2,1,0:T(8,128)(2,1)S(1)} %get-tuple-element.59.highs, bf16[4,256,128]{2,1,0:T(8,128)(2,1)S(1)} %get-tuple-element.60.lows, ...), custom_call_target="tpu_custom_call" | custom-call | flops 134217728 | bytes 524288 | tf_op jit(solution)/shard_map/pallas_call | solution.py:17
  21.9 0.1 collective-permute-done.3.rest_0_
  22.0 0.6 %shard_map.102 = (f32[128,256]{1,0:T(8,128)S(1)}, f32[256,128]{1,0:T(8,128)S(1)}) custom-call(bf16[4,2048,256]{2,1,0:T(8,128)(2,1)S(1)} %get-tuple-element.57.masked, bf16[4,128,2048]{2,1,0:T(8,128)(2,1)S(1)} %get-tuple-element.58.turned, bf16[4,256,128]{2,1,0:T(8,128)(2,1)S(1)} %get-tuple-element.59.highs, bf16[4,256,128]{2,1,0:T(8,128)(2,1)S(1)} %get-tuple-element.60.lows, ...), custom_call_target="tpu_custom_call" | custom-call | flops 134217728 | bytes 524288 | tf_op jit(solution)/shard_map/pallas_call | solution.py:17
  22.6 0.0 collective-permute-done.5.rest_0_
  22.6 0.6 %shard_map.103 = (f32[4,64,128]{2,1,0:T(8,128)S(1)}, f32[4,64,128]{2,1,0:T(8,128)S(1)}) custom-call(bf16[4,2048,256]{2,1,0:T(8,128)(2,1)S(1)} %get-tuple-element.57.masked, bf16[4,128,2048]{2,1,0:T(8,128)(2,1)S(1)} %get-tuple-element.58.turned, bf16[4,256,128]{2,1,0:T(8,128)(2,1)S(1)} %get-tuple-element.59.highs, ...), custom_call_target="tpu_custom_call" | custom-call | flops 134217728 | bytes 524288 | tf_op jit(solution)/shard_map/pallas_call | solution.py:17
  23.2 0.1 collective-permute-start.6
  23.3 1.3 %collective-permute-done.6.came = f32[4,64,128]{2,1,0:T(8,128)S(1)} collective-permute-done((f32[4,64,128]{2,1,0:T(8,128)S(1)}, f32[4,64,128]{2,1,0:T(8,128)S(1)}, u32[]{:S(2)}, u32[]{:S(2)}) %collective-permute-start.6) | collective-permute-done | bytes 131104 | tf_op jit(solution)/shard_map/ppermute | solution.py:225
  24.6 2.5 %collective-permute-start.7 = (f32[64,128]{1,0:T(8,128)S(1)}, f32[64,128]{1,0:T(8,128)S(1)}, u32[]{:S(2)}, u32[]{:S(2)}) collective-permute-start(f32[64,128]{1,0:T(8,128)S(1)} %get-tuple-element.73), channel_id=1, source_target_pairs={{0,24},{4,28},{8,16},{12,20},{16,8},{20,12},{24,0},{28,4},{1,25},{... | collective-permute-start | bytes 98312 | tf_op jit(solution)/shard_map/ppermute | solution.py:225
  27.1 0.5 %collective-permute-start.8 = (f32[64,128]{1,0:T(8,128)S(1)}, f32[64,128]{1,0:T(8,128)S(1)}, u32[]{:S(2)}, u32[]{:S(2)}) collective-permute-start(f32[64,128]{1,0:T(8,128)S(1)} %get-tuple-element.74), channel_id=1, source_target_pairs={{0,16},{4,20},{8,24},{12,28},{16,0},{20,4},{24,8},{28,12},{1,17},{... | collective-permute-start | bytes 98312 | tf_op jit(solution)/shard_map/ppermute | solution.py:225
  27.6 0.6 %collective-permute-start.9 = (f32[64,128]{1,0:T(8,128)S(1)}, f32[64,128]{1,0:T(8,128)S(1)}, u32[]{:S(2)}, u32[]{:S(2)}) collective-permute-start(f32[64,128]{1,0:T(8,128)S(1)} %get-tuple-element.75), channel_id=1, source_target_pairs={{0,8},{4,12},{8,0},{12,4},{16,24},{20,28},{24,16},{28,20},{1,9},{5... | collective-permute-start | bytes 98312 | tf_op jit(solution)/shard_map/ppermute | solution.py:225
  28.2 0.6 %shard_map.98 = f32[128,128]{1,0:T(8,128)} custom-call(f32[128,128]{1,0:T(8,128)S(1)} %get-tuple-element.52.value), custom_call_target="tpu_custom_call" | custom-call | tf_op jit(solution)/shard_map/pallas_call | solution.py:17
  28.8 0.7 %collective-permute-done.7.refs_0_ = f32[64,128]{1,0:T(8,128)S(1)} collective-permute-done((f32[64,128]{1,0:T(8,128)S(1)}, f32[64,128]{1,0:T(8,128)S(1)}, u32[]{:S(2)}, u32[]{:S(2)}) %collective-permute-start.7) | collective-permute-done | bytes 32800 | tf_op jit(solution)/shard_map/ppermute | solution.py:225
  29.5 1.5 %collective-permute-done.8.refs_1_ = f32[64,128]{1,0:T(8,128)S(1)} collective-permute-done((f32[64,128]{1,0:T(8,128)S(1)}, f32[64,128]{1,0:T(8,128)S(1)}, u32[]{:S(2)}, u32[]{:S(2)}) %collective-permute-start.8) | collective-permute-done | bytes 32800 | tf_op jit(solution)/shard_map/ppermute | solution.py:225
  31.1 0.5 %collective-permute-done.9.refs_2_ = f32[64,128]{1,0:T(8,128)S(1)} collective-permute-done((f32[64,128]{1,0:T(8,128)S(1)}, f32[64,128]{1,0:T(8,128)S(1)}, u32[]{:S(2)}, u32[]{:S(2)}) %collective-permute-start.9) | collective-permute-done | bytes 32800 | tf_op jit(solution)/shard_map/ppermute | solution.py:225
  31.5 0.6 %shard_map.105 = (f32[1,16,256]{2,1,0:T(8,128)}, f32[1,32,128]{2,1,0:T(8,128)}) custom-call(f32[64,128]{1,0:T(8,128)S(1)} %collective-permute-done.7.refs_0_, f32[64,128]{1,0:T(8,128)S(1)} %collective-permute-done.8.refs_1_, f32[64,128]{1,0:T(8,128)S(1)} %collective-permute-done.9.refs_2_, f32[64,128]{1,0:T(8,128)S(1)} %get-tuple-element.76.refs_3_), custom_call_target="tpu_custom_call" | custom-call | tf_op jit(solution)/shard_map/pallas_call | solution.py:17
  (1 shorter events, 0.0 us)
Async XLA Ops:
  2.5 7.8 %collective-permute-start.1 = (f32[129,1,128]{2,1,0:T(1,128)S(1)}, f32[129,1,128]{2,1,0:T(1,128)S(1)}, u32[]{:S(2)}, u32[]{:S(2)}) collective-permute-start(f32[129,1,128]{2,1,0:T(1,128)S(1)} %get-tuple-element.50), channel_id=1, source_target_pairs={{0,2},{1,3},{2,0},{3,1},{4,6},{5,7},{6,4},{7,5},{8,10},{9,11},{10,... | collective-permute-start | bytes 198152 | tf_op jit(solution)/shard_map/ppermute | solution.py:225
  7.2 6.8 %collective-permute-start.2 = (f32[129,1,128]{2,1,0:T(1,128)S(1)}, f32[129,1,128]{2,1,0:T(1,128)S(1)}, u32[]{:S(2)}, u32[]{:S(2)}) collective-permute-start(f32[129,1,128]{2,1,0:T(1,128)S(1)} %get-tuple-element.51), channel_id=1, source_target_pairs={{0,3},{1,2},{2,1},{3,0},{4,7},{5,6},{6,5},{7,4},{8,11},{9,10},{10,... | collective-permute-start | bytes 198152 | tf_op jit(solution)/shard_map/ppermute | solution.py:225
  9.6 4.7 %collective-permute-start = (f32[129,1,128]{2,1,0:T(1,128)S(1)}, f32[129,1,128]{2,1,0:T(1,128)S(1)}, u32[]{:S(2)}, u32[]{:S(2)}) collective-permute-start(f32[129,1,128]{2,1,0:T(1,128)S(1)} %get-tuple-element.49), channel_id=1, source_target_pairs={{0,1},{1,0},{2,3},{3,2},{4,5},{5,4},{6,7},{7,6},{8,9},{9,8},{10,11... | collective-permute-start | bytes 198152 | tf_op jit(solution)/shard_map/ppermute | solution.py:225
  14.6 6.7 %collective-permute-start.4 = (f32[128,128]{1,0:T(8,128)S(1)}, f32[128,128]{1,0:T(8,128)S(1)}, u32[]{:S(2)}, u32[]{:S(2)}) collective-permute-start(f32[128,128]{1,0:T(8,128)S(1)} %get-tuple-element.62), channel_id=1, source_target_pairs={{0,3},{1,2},{2,1},{3,0},{4,7},{5,6},{6,5},{7,4},{8,11},{9,10},{10,... | collective-permute-start | bytes 196616 | tf_op jit(solution)/shard_map/ppermute | solution.py:225
  16.9 5.1 %collective-permute-start.3 = (f32[128,128]{1,0:T(8,128)S(1)}, f32[128,128]{1,0:T(8,128)S(1)}, u32[]{:S(2)}, u32[]{:S(2)}) collective-permute-start(f32[128,128]{1,0:T(8,128)S(1)} %get-tuple-element.61), channel_id=1, source_target_pairs={{0,1},{1,0},{2,3},{3,2},{4,5},{5,4},{6,7},{7,6},{8,9},{9,8},{10,11... | collective-permute-start | bytes 196616 | tf_op jit(solution)/shard_map/ppermute | solution.py:225
  16.9 5.7 %collective-permute-start.5 = (f32[128,128]{1,0:T(8,128)S(1)}, f32[128,128]{1,0:T(8,128)S(1)}, u32[]{:S(2)}, u32[]{:S(2)}) collective-permute-start(f32[128,128]{1,0:T(8,128)S(1)} %get-tuple-element.70), channel_id=1, source_target_pairs={{0,2},{1,3},{2,0},{3,1},{4,6},{5,7},{6,4},{7,5},{8,10},{9,11},{10,... | collective-permute-start | bytes 196616 | tf_op jit(solution)/shard_map/ppermute | solution.py:225
  23.2 1.4 %collective-permute-start.6 = (f32[4,64,128]{2,1,0:T(8,128)S(1)}, f32[4,64,128]{2,1,0:T(8,128)S(1)}, u32[]{:S(2)}, u32[]{:S(2)}) collective-permute-start(f32[4,64,128]{2,1,0:T(8,128)S(1)} %get-tuple-element.72), channel_id=1, source_target_pairs={{0,4},{4,0},{8,12},{12,8},{16,20},{20,16},{24,28},{28,24},{1,5},{5... | collective-permute-start | bytes 393224 | tf_op jit(solution)/shard_map/ppermute | solution.py:225
  24.6 4.9 %collective-permute-start.7 = (f32[64,128]{1,0:T(8,128)S(1)}, f32[64,128]{1,0:T(8,128)S(1)}, u32[]{:S(2)}, u32[]{:S(2)}) collective-permute-start(f32[64,128]{1,0:T(8,128)S(1)} %get-tuple-element.73), channel_id=1, source_target_pairs={{0,24},{4,28},{8,16},{12,20},{16,8},{20,12},{24,0},{28,4},{1,25},{... | collective-permute-start | bytes 98312 | tf_op jit(solution)/shard_map/ppermute | solution.py:225
  27.1 3.9 %collective-permute-start.8 = (f32[64,128]{1,0:T(8,128)S(1)}, f32[64,128]{1,0:T(8,128)S(1)}, u32[]{:S(2)}, u32[]{:S(2)}) collective-permute-start(f32[64,128]{1,0:T(8,128)S(1)} %get-tuple-element.74), channel_id=1, source_target_pairs={{0,16},{4,20},{8,24},{12,28},{16,0},{20,4},{24,8},{28,12},{1,17},{... | collective-permute-start | bytes 98312 | tf_op jit(solution)/shard_map/ppermute | solution.py:225
  27.6 3.9 %collective-permute-start.9 = (f32[64,128]{1,0:T(8,128)S(1)}, f32[64,128]{1,0:T(8,128)S(1)}, u32[]{:S(2)}, u32[]{:S(2)}) collective-permute-start(f32[64,128]{1,0:T(8,128)S(1)} %get-tuple-element.75), channel_id=1, source_target_pairs={{0,8},{4,12},{8,0},{12,4},{16,24},{20,28},{24,16},{28,20},{1,9},{5... | collective-permute-start | bytes 98312 | tf_op jit(solution)/shard_map/ppermute | solution.py:225
